TPU v7x, 512 devices: a whole 4x8x8 slice. The times are simulated.
512 devices in a mesh: depth: 64 (over y, x, core), rows: 8 (over z).
Axes of the slice: x: 4, y: 8, z: 8, core: 2. Of those that a mesh axis runs over, the one named last changes fastest.
Arguments:
- substrate: float32 [256, 128, 1024], P('depth', 'rows'), may hold values from 0.2 to 1
- catalyst: float32 [256, 128, 1024], P('depth', 'rows'), may hold values from 0 to 0.5
- feed_rate: float32 [256, 128, 1024], P('depth', 'rows'), may hold values from 0.01 to 0.1
- kill_rate: float32 [256, 128, 1024], P('depth', 'rows'), may hold values from 0.03 to 0.1
- extinction: float32 [256, 128, 1024], P('depth', 'rows'), may hold values from 0.001 to 0.03
- palette: float32 [3, 3], replicated, may hold values from -2 to 2
Outputs:
- new_substrate: float32 [256, 128, 1024], P('depth', 'rows')
- new_catalyst: float32 [256, 128, 1024], P('depth', 'rows')
- image: float32 [4, 128, 1024], P(None, 'rows', 'depth')
All inputs are finite; a program needn't handle non-finite values.
Results may differ from a plain program's by a relative error of at most 0.000039.
Values sent between devices are 32-bit elements; how exact they have to be, the bound alone decides.
A program may use at most 64 MiB of HBM per device.

v0:
```python
import jax
import jax.numpy as jnp
from jax import lax
from jax.sharding import PartitionSpec as P

STEPS = 2


diffusion_fast = 0.08
diffusion_slow = 0.04
time_step = 2.0


def extended(shard, sides, width):
    edges = {}
    for axis, dim in sides:
        size, length = (lax.axis_size(axis), shard.shape[dim])
        up = [(i, (i + 1) % size) for i in range(size - 1)]
        last = lax.slice_in_dim(shard, length - width, length, axis=dim)
        first = lax.slice_in_dim(shard, 0, width, axis=dim)
        edges[dim] = (
            lax.ppermute(last, axis, up),
            lax.ppermute(first, axis, [(b, a) for a, b in up]),
        )
    done = []
    for _, dim in sides:
        low, high = edges[dim]
        around = [(width, width) if d in done else (0, 0) for d in range(shard.ndim)]
        shard = jnp.concatenate([jnp.pad(low, around), shard, jnp.pad(high, around)], axis=dim)
        done.append(dim)
    return shard


def swapped(value, axis, distance):
    mask = 2**distance
    pairs = [(source, source ^ mask) for source in range(lax.axis_size(axis))]
    return lax.ppermute(value, axis, pairs)


def react(padded, feed, kill):
    center = padded[:, 1:-1, 1:-1]
    column_pad = jnp.pad(center, ((0, 0), (0, 0), (0, 0), (1, 1)))
    laplace = (
        padded[:, 2:, 1:-1] + padded[:, :-2, 1:-1] + padded[:, 1:-1, 2:] + padded[:, 1:-1, :-2]
    )
    laplace = laplace + column_pad[..., 2:] + column_pad[..., :-2] - 6.0 * center
    fed = center[0]
    auto = center[1]
    reaction = fed * auto * auto
    fed_change = diffusion_fast * laplace[0] - reaction + feed * (1.0 - fed)
    auto_change = diffusion_slow * laplace[1] + reaction - (feed + kill) * auto
    return jnp.stack([fed + time_step * fed_change, auto + time_step * auto_change])


def advance(fields, feed, kill):
    padded = extended(fields, (("depth", 1), ("rows", 2)), 1)
    return react(padded, feed, kill)


def body(substrate, catalyst, feed_rate, kill_rate, extinction, palette):
    row_cells = substrate.shape[1]
    fields = jnp.stack([substrate, catalyst])
    for iteration in range(STEPS):
        fields = advance(fields, feed_rate, kill_rate)
    fed = fields[0]
    auto = fields[1]
    passing = jnp.exp(-extinction * (0.25 + 4.0 * auto * auto))
    opacity = 1.0 - passing
    colors = jax.nn.sigmoid(
        8.0 * palette[:, 0, None, None, None] * (fed - 0.65)[None]
        + 8.0 * palette[:, 1, None, None, None] * (auto - 0.25)[None]
        + palette[:, 2, None, None, None]
    )
    cumul = jnp.cumprod(passing, axis=0)
    before = jnp.concatenate([jnp.ones_like(passing[:1]), cumul[:-1]], axis=0)
    weights = before * opacity
    partial_value = jnp.stack(
        [
            jnp.sum(weights * colors[0], axis=0),
            jnp.sum(weights * colors[1], axis=0),
            jnp.sum(weights * colors[2], axis=0),
            cumul[-1],
        ]
    )
    count = lax.axis_size("depth")
    levels = count.bit_length() - 1
    columns = partial_value.shape[2]
    block = columns // count
    shaped = partial_value.reshape((4, row_cells) + (2,) * levels + (block,))
    order = (0, 1) + tuple(range(levels + 1, 1, -1)) + (levels + 2,)
    partial_value = jnp.transpose(shaped, order).reshape((4, row_cells, columns))
    position = lax.axis_index("depth")
    for level in range(levels):
        half = partial_value.shape[2] // 2
        mine_bit = position >> level & 1
        kept = lax.dynamic_slice_in_dim(partial_value, mine_bit * half, half, 2)
        given = lax.dynamic_slice_in_dim(partial_value, (1 - mine_bit) * half, half, 2)
        other = swapped(given, "depth", level)
        is_front = mine_bit == 0
        nearer = jnp.where(is_front, kept, other)
        farther = jnp.where(is_front, other, kept)
        partial_value = jnp.concatenate(
            [nearer[:3] + nearer[3:] * farther[:3], nearer[3:] * farther[3:]], axis=0
        )
    image = jnp.concatenate([partial_value[:3], 1.0 - partial_value[3:]], axis=0)
    return (fed, auto, image)


def solution(mesh):
    return jax.shard_map(
        body,
        mesh=mesh,
        in_specs=(
            P("depth", "rows", None),
            P("depth", "rows", None),
            P("depth", "rows", None),
            P("depth", "rows", None),
            P("depth", "rows", None),
            P(),
        ),
        out_specs=(P("depth", "rows", None), P("depth", "rows", None), P(None, "rows", "depth")),
        check_vma=False,
    )
```

profile of v0, /device:TPU:222, one launch (start us, length us, event | category | flops | bytes accessed | tf_op | source)
XLA Modules:
  0.0 89.4 jit_solution(175547273740199745)
XLA Ops:
  0.6 0.0 copy-start.1
  0.6 0.0 copy-start
  0.7 0.0 copy-start.6
  0.7 0.0 copy-start.3
  0.7 0.0 copy-start.5
  0.7 1.0 %fusion.48 = (f32[2,1,16,1024]{3,2,1,0:T(8,128)S(1)}, f32[2,1,16,1024]{3,2,1,0:T(8,128)S(1)}) fusion(f32[1,4,16,1024]{3,2,1,0:T(8,128)} %bitcast.90, f32[1,4,16,1024]{3,2,1,0:T(8,128)} %bitcast.86), kind=kLoop, calls=%fused_computation.113 | loop fusion | flops 65536 | bytes 786432 | tf_op jit(solution)/shard_map/stack | solution.py:62
  1.7 2.2 %collective-permute-start = (f32[2,1,16,1024]{3,2,1,0:T(8,128)S(1)}, f32[2,1,16,1024]{3,2,1,0:T(8,128)S(1)}, u32[]{:S(2)}, u32[]{:S(2)}) collective-permute-start(f32[2,1,16,1024]{3,2,1,0:T(8,128)S(1)} %get-tuple-element.25), channel_id=1, source_target_pairs={{8,0},{16,8},{24,16},{32,24},{40,32},{48,40},{56,48},{64,56},{72,6... | collective-permute-start | bytes 393224 | tf_op jit(solution)/shard_map/ppermute | solution.py:23
  3.9 2.2 %collective-permute-start.1 = (f32[2,1,16,1024]{3,2,1,0:T(8,128)S(1)}, f32[2,1,16,1024]{3,2,1,0:T(8,128)S(1)}, u32[]{:S(2)}, u32[]{:S(2)}) collective-permute-start(f32[2,1,16,1024]{3,2,1,0:T(8,128)S(1)} %get-tuple-element.24), channel_id=1, source_target_pairs={{0,8},{8,16},{16,24},{24,32},{32,40},{40,48},{48,56},{56,64},{64,7... | collective-permute-start | bytes 393224 | tf_op jit(solution)/shard_map/ppermute | solution.py:22
  6.1 1.1 %fusion.57 = (f32[2,4,1,1024]{3,2,1,0:T(1,128)S(1)}, f32[2,4,1,1024]{3,2,1,0:T(1,128)S(1)}) fusion(f32[1,4,16,1024]{3,2,1,0:T(8,128)} %bitcast.91, f32[1,4,16,1024]{3,2,1,0:T(8,128)} %bitcast.87), kind=kLoop, calls=%fused_computation.143 | loop fusion | flops 16384 | bytes 589824 | tf_op jit(solution)/shard_map/stack | solution.py:62
  7.2 1.9 %collective-permute-start.2 = (f32[2,4,1,1024]{3,2,1,0:T(1,128)S(1)}, f32[2,4,1,1024]{3,2,1,0:T(1,128)S(1)}, u32[]{:S(2)}, u32[]{:S(2)}) collective-permute-start(f32[2,4,1,1024]{3,2,1,0:T(1,128)S(1)} %get-tuple-element.22), channel_id=1, source_target_pairs={{1,0},{2,1},{3,2},{4,3},{5,4},{6,5},{7,6},{9,8},{10,9},{11,10},{12... | collective-permute-start | bytes 98312 | tf_op jit(solution)/shard_map/ppermute | solution.py:23
  9.1 5.5 %collective-permute-start.3 = (f32[2,4,1,1024]{3,2,1,0:T(1,128)S(1)}, f32[2,4,1,1024]{3,2,1,0:T(1,128)S(1)}, u32[]{:S(2)}, u32[]{:S(2)}) collective-permute-start(f32[2,4,1,1024]{3,2,1,0:T(1,128)S(1)} %get-tuple-element.23), channel_id=1, source_target_pairs={{0,1},{1,2},{2,3},{3,4},{4,5},{5,6},{6,7},{8,9},{9,10},{10,11},{11... | collective-permute-start | bytes 98312 | tf_op jit(solution)/shard_map/ppermute | solution.py:22
  14.6 1.1 %pad_maximum_fusion = f32[2,4,16,1024]{3,2,1,0:T(8,128)S(1)} fusion(f32[1,4,16,1024]{3,2,1,0:T(8,128)} %bitcast.88, f32[1,4,16,1024]{3,2,1,0:T(8,128)} %bitcast.92), kind=kLoop, calls=%fused_computation.5 | loop fusion | flops 131072 | bytes 1048576 | tf_op jit(solution)/shard_map/stack | solution.py:62
  15.7 0.0 copy-done.6
  15.7 0.2 multiply_reduce_fusion.1
  15.9 0.0 collective-permute-done.2
  15.9 0.3 collective-permute-done.3
  16.2 0.0 collective-permute-done
  16.2 0.0 collective-permute-done.1
  16.2 0.0 copy-done.1
  16.2 0.0 copy-done
  16.2 0.4 fusion.2
  16.7 0.0 copy-done.3
  16.7 0.0 copy-done.5
  16.7 0.2 fusion.39
  16.9 2.9 %collective-permute-start.4 = (f32[2,1,16,1024]{3,2,1,0:T(8,128)S(1)}, f32[2,1,16,1024]{3,2,1,0:T(8,128)S(1)}, u32[]{:S(2)}, u32[]{:S(2)}) collective-permute-start(f32[2,1,16,1024]{3,2,1,0:T(8,128)S(1)} %get-tuple-element.21), channel_id=1, source_target_pairs={{8,0},{16,8},{24,16},{32,24},{40,32},{48,40},{56,48},{64,56},{72,6... | collective-permute-start | bytes 393224 | tf_op jit(solution)/shard_map/ppermute | solution.py:23
  19.8 4.8 %collective-permute-start.5 = (f32[2,1,16,1024]{3,2,1,0:T(8,128)S(1)}, f32[2,1,16,1024]{3,2,1,0:T(8,128)S(1)}, u32[]{:S(2)}, u32[]{:S(2)}) collective-permute-start(f32[2,1,16,1024]{3,2,1,0:T(8,128)S(1)} %get-tuple-element.20), channel_id=1, source_target_pairs={{0,8},{8,16},{16,24},{24,32},{32,40},{40,48},{48,56},{56,64},{64,7... | collective-permute-start | bytes 393224 | tf_op jit(solution)/shard_map/ppermute | solution.py:22
  24.6 1.9 %collective-permute-start.6 = (f32[2,4,1,1024]{3,2,1,0:T(1,128)S(1)}, f32[2,4,1,1024]{3,2,1,0:T(1,128)S(1)}, u32[]{:S(2)}, u32[]{:S(2)}) collective-permute-start(f32[2,4,1,1024]{3,2,1,0:T(1,128)S(1)} %get-tuple-element.18), channel_id=1, source_target_pairs={{1,0},{2,1},{3,2},{4,3},{5,4},{6,5},{7,6},{9,8},{10,9},{11,10},{12... | collective-permute-start | bytes 98312 | tf_op jit(solution)/shard_map/ppermute | solution.py:23
  26.6 5.1 %collective-permute-start.7 = (f32[2,4,1,1024]{3,2,1,0:T(1,128)S(1)}, f32[2,4,1,1024]{3,2,1,0:T(1,128)S(1)}, u32[]{:S(2)}, u32[]{:S(2)}) collective-permute-start(f32[2,4,1,1024]{3,2,1,0:T(1,128)S(1)} %get-tuple-element.19), channel_id=1, source_target_pairs={{0,1},{1,2},{2,3},{3,4},{4,5},{5,6},{6,7},{8,9},{9,10},{10,11},{11... | collective-permute-start | bytes 98312 | tf_op jit(solution)/shard_map/ppermute | solution.py:22
  31.8 0.0 copy-start.4
  31.8 0.0 collective-permute-done.6
  31.8 1.5 %collective-permute-done.7 = f32[2,4,1,1024]{3,2,1,0:T(1,128)S(1)} collective-permute-done((f32[2,4,1,1024]{3,2,1,0:T(1,128)S(1)}, f32[2,4,1,1024]{3,2,1,0:T(1,128)S(1)}, u32[]{:S(2)}, u32[]{:S(2)}) %collective-permute-start.7) | collective-permute-done | bytes 32800 | tf_op jit(solution)/shard_map/ppermute | solution.py:22
  33.3 0.0 collective-permute-done.4
  33.3 0.0 collective-permute-done.5
  33.3 0.5 fusion.5
  33.7 0.9 broadcast_add_fusion
  34.6 0.3 fusion.53
  34.9 0.3 add_divide_fusion
  35.2 0.1 fusion.24
  35.4 0.7 stack.38
  36.1 0.7 stack.39
  36.8 0.7 stack.40
  37.5 0.7 stack.41
  38.2 1.7 %maximum_bitcast_fusion = f32[4,16,2,2,2,2,2,2,16]{8,2,3,4,5,6,7,1,0:T(2,128)S(1)} fusion(f32[1,16,2,2,2,2,2,2,16]{8,7,6,5,4,3,2,1,0:T(2,128)S(1)} %stack.41, f32[1,16,2,2,2,2,2,2,16]{8,7,6,5,4,3,2,1,0:T(2,128)S(1)} %stack.40, f32[1,16,2,2,2,2,2,2,16]{8,7,6,5,4,3,2,1,0:T(2,128)S(1)} %stack.39, f32[1,16,2,2,2,2,2,2,16]{8,7,6,5,4,3,2,1,0:T(2,128)S(1)} %stack.38), kind=kLoop, calls=%fused_computation | loop fusion | flops 196608 | bytes 524288 | tf_op jit(solution)/shard_map/transpose | solution.py:91
  40.0 1.9 %copy.10 = f32[4,16,2,2,2,2,2,2,16]{8,7,6,5,4,3,2,1,0:T(2,128)S(1)} copy(f32[4,16,2,2,2,2,2,2,16]{8,2,3,4,5,6,7,1,0:T(2,128)S(1)} %maximum_bitcast_fusion) | data formatting | bytes 524288 | tf_op jit(solution)/shard_map/transpose | solution.py:91
  41.9 3.1 %reshape.46 = f32[4,16,1024]{2,1,0:T(8,128)S(1)} reshape(f32[4,16,2,2,2,2,2,2,16]{8,7,6,5,4,3,2,1,0:T(2,128)S(1)} %copy.10) | data formatting | bytes 524288 | tf_op jit(solution)/shard_map/reshape | solution.py:91
  45.0 5.8 %collective-permute-start.8 = (f32[4,16,512]{2,1,0:T(8,128)S(1)}, f32[4,16,512]{2,1,0:T(8,128)S(1)}, u32[]{:S(2)}, u32[]{:S(2)}) collective-permute-start(f32[4,16,512]{2,1,0:T(8,128)S(1)} %constant_dynamic-slice_fusion), channel_id=1, source_target_pairs={{0,8},{8,0},{16,24},{24,16},{32,40},{40,32},{48,56},{56,48},{64,72... | collective-permute-start | bytes 393224 | tf_op jit(solution)/shard_map/ppermute | solution.py:37
  50.9 1.0 %collective-permute-done.8 = f32[4,16,512]{2,1,0:T(8,128)S(1)} collective-permute-done((f32[4,16,512]{2,1,0:T(8,128)S(1)}, f32[4,16,512]{2,1,0:T(8,128)S(1)}, u32[]{:S(2)}, u32[]{:S(2)}) %collective-permute-start.8) | collective-permute-done | bytes 131104 | tf_op jit(solution)/shard_map/ppermute | solution.py:37
  51.9 1.9 %collective-permute-start.9 = (f32[4,16,256]{2,1,0:T(8,128)S(1)}, f32[4,16,256]{2,1,0:T(8,128)S(1)}, u32[]{:S(2)}, u32[]{:S(2)}) collective-permute-start(f32[4,16,256]{2,1,0:T(8,128)S(1)} %fusion.50), channel_id=1, source_target_pairs={{0,16},{8,24},{16,0},{24,8},{32,48},{40,56},{48,32},{56,40},{64,80... | collective-permute-start | bytes 196616 | tf_op jit(solution)/shard_map/ppermute | solution.py:37
  53.9 4.3 %collective-permute-done.9 = f32[4,16,256]{2,1,0:T(8,128)S(1)} collective-permute-done((f32[4,16,256]{2,1,0:T(8,128)S(1)}, f32[4,16,256]{2,1,0:T(8,128)S(1)}, u32[]{:S(2)}, u32[]{:S(2)}) %collective-permute-start.9) | collective-permute-done | bytes 65568 | tf_op jit(solution)/shard_map/ppermute | solution.py:37
  58.3 1.9 %collective-permute-start.10 = (f32[4,16,128]{2,1,0:T(8,128)S(1)}, f32[4,16,128]{2,1,0:T(8,128)S(1)}, u32[]{:S(2)}, u32[]{:S(2)}) collective-permute-start(f32[4,16,128]{2,1,0:T(8,128)S(1)} %fusion.65), channel_id=1, source_target_pairs={{0,32},{8,40},{16,48},{24,56},{32,0},{40,8},{48,16},{56,24},{64,96... | collective-permute-start | bytes 98312 | tf_op jit(solution)/shard_map/ppermute | solution.py:37
  60.2 5.4 %collective-permute-done.10 = f32[4,16,128]{2,1,0:T(8,128)S(1)} collective-permute-done((f32[4,16,128]{2,1,0:T(8,128)S(1)}, f32[4,16,128]{2,1,0:T(8,128)S(1)}, u32[]{:S(2)}, u32[]{:S(2)}) %collective-permute-start.10) | collective-permute-done | bytes 32800 | tf_op jit(solution)/shard_map/ppermute | solution.py:37
  65.6 0.1 fusion.63
  65.7 1.9 %collective-permute-start.11 = (f32[4,16,64]{2,1,0:T(8,128)S(1)}, f32[4,16,64]{2,1,0:T(8,128)S(1)}, u32[]{:S(2)}, u32[]{:S(2)}) collective-permute-start(f32[4,16,64]{2,1,0:T(8,128)S(1)} %fusion.63), channel_id=1, source_target_pairs={{0,64},{8,72},{16,80},{24,88},{32,96},{40,104},{48,112},{56,120},{... | collective-permute-start | bytes 49160 | tf_op jit(solution)/shard_map/ppermute | solution.py:37
  67.6 3.9 %collective-permute-done.11 = f32[4,16,64]{2,1,0:T(8,128)S(1)} collective-permute-done((f32[4,16,64]{2,1,0:T(8,128)S(1)}, f32[4,16,64]{2,1,0:T(8,128)S(1)}, u32[]{:S(2)}, u32[]{:S(2)}) %collective-permute-start.11) | collective-permute-done | bytes 16416 | tf_op jit(solution)/shard_map/ppermute | solution.py:37
  71.5 0.1 broadcast_select_fusion.5
  71.6 0.1 fusion.61
  71.7 1.9 %collective-permute-start.12 = (f32[4,16,32]{2,1,0:T(8,128)S(1)}, f32[4,16,32]{2,1,0:T(8,128)S(1)}, u32[]{:S(2)}, u32[]{:S(2)}) collective-permute-start(f32[4,16,32]{2,1,0:T(8,128)S(1)} %fusion.61), channel_id=1, source_target_pairs={{0,128},{8,136},{16,144},{24,152},{32,160},{40,168},{48,176},{56,1... | collective-permute-start | bytes 24584 | tf_op jit(solution)/shard_map/ppermute | solution.py:37
  73.6 4.8 %collective-permute-done.12 = f32[4,16,32]{2,1,0:T(8,128)S(1)} collective-permute-done((f32[4,16,32]{2,1,0:T(8,128)S(1)}, f32[4,16,32]{2,1,0:T(8,128)S(1)}, u32[]{:S(2)}, u32[]{:S(2)}) %collective-permute-start.12) | collective-permute-done | bytes 8224 | tf_op jit(solution)/shard_map/ppermute | solution.py:37
  78.4 0.1 broadcast_select_fusion.7
  78.5 0.1 fusion.59
  78.6 1.9 %collective-permute-start.13 = (f32[4,16,16]{2,1,0:T(8,128)S(1)}, f32[4,16,16]{2,1,0:T(8,128)S(1)}, u32[]{:S(2)}, u32[]{:S(2)}) collective-permute-start(f32[4,16,16]{2,1,0:T(8,128)S(1)} %fusion.59), channel_id=1, source_target_pairs={{0,256},{8,264},{16,272},{24,280},{32,288},{40,296},{48,304},{56,3... | collective-permute-start | bytes 12296 | tf_op jit(solution)/shard_map/ppermute | solution.py:37
  80.5 8.1 %collective-permute-done.13 = f32[4,16,16]{2,1,0:T(8,128)S(1)} collective-permute-done((f32[4,16,16]{2,1,0:T(8,128)S(1)}, f32[4,16,16]{2,1,0:T(8,128)S(1)}, u32[]{:S(2)}, u32[]{:S(2)}) %collective-permute-start.13) | collective-permute-done | bytes 4128 | tf_op jit(solution)/shard_map/ppermute | solution.py:37
  88.6 0.1 broadcast_select_fusion.9
  88.8 0.6 pad_maximum_fusion.22
  (26 shorter events, 0.3 us)
Async XLA Ops:
  0.6 15.6 %copy-start.1 = (f32[4,16,1024]{2,1,0:T(8,128)S(1)}, f32[4,16,1024]{2,1,0:T(8,128)}, u32[]{:S(2)}) copy-start(f32[4,16,1024]{2,1,0:T(8,128)} %param.6) | copy-start | bytes 786436
  0.6 15.6 %copy-start = (f32[4,16,1024]{2,1,0:T(8,128)S(1)}, f32[4,16,1024]{2,1,0:T(8,128)}, u32[]{:S(2)}) copy-start(f32[4,16,1024]{2,1,0:T(8,128)} %param.7) | copy-start | bytes 786436
  0.7 15.1 %copy-start.6 = (f32[3,3]{1,0:T(4,128)S(1)}, f32[3,3]{1,0:T(4,128)}, u32[]{:S(2)}) copy-start(f32[3,3]{1,0:T(4,128)} %param.11) | copy-start | bytes 112
  0.7 16.0 %copy-start.3 = (f32[4,16,1024]{2,1,0:T(8,128)S(1)}, f32[4,16,1024]{2,1,0:T(8,128)}, u32[]{:S(2)}) copy-start(f32[4,16,1024]{2,1,0:T(8,128)} %param.8) | copy-start | bytes 786436
  0.7 16.0 %copy-start.5 = (f32[4,16,1024]{2,1,0:T(8,128)S(1)}, f32[4,16,1024]{2,1,0:T(8,128)}, u32[]{:S(2)}) copy-start(f32[4,16,1024]{2,1,0:T(8,128)} %param.9) | copy-start | bytes 786436
  1.7 14.5 %collective-permute-start = (f32[2,1,16,1024]{3,2,1,0:T(8,128)S(1)}, f32[2,1,16,1024]{3,2,1,0:T(8,128)S(1)}, u32[]{:S(2)}, u32[]{:S(2)}) collective-permute-start(f32[2,1,16,1024]{3,2,1,0:T(8,128)S(1)} %get-tuple-element.25), channel_id=1, source_target_pairs={{8,0},{16,8},{24,16},{32,24},{40,32},{48,40},{56,48},{64,56},{72,6... | collective-permute-start | bytes 393224 | tf_op jit(solution)/shard_map/ppermute | solution.py:23
  3.9 12.3 %collective-permute-start.1 = (f32[2,1,16,1024]{3,2,1,0:T(8,128)S(1)}, f32[2,1,16,1024]{3,2,1,0:T(8,128)S(1)}, u32[]{:S(2)}, u32[]{:S(2)}) collective-permute-start(f32[2,1,16,1024]{3,2,1,0:T(8,128)S(1)} %get-tuple-element.24), channel_id=1, source_target_pairs={{0,8},{8,16},{16,24},{24,32},{32,40},{40,48},{48,56},{56,64},{64,7... | collective-permute-start | bytes 393224 | tf_op jit(solution)/shard_map/ppermute | solution.py:22
  7.2 8.7 %collective-permute-start.2 = (f32[2,4,1,1024]{3,2,1,0:T(1,128)S(1)}, f32[2,4,1,1024]{3,2,1,0:T(1,128)S(1)}, u32[]{:S(2)}, u32[]{:S(2)}) collective-permute-start(f32[2,4,1,1024]{3,2,1,0:T(1,128)S(1)} %get-tuple-element.22), channel_id=1, source_target_pairs={{1,0},{2,1},{3,2},{4,3},{5,4},{6,5},{7,6},{9,8},{10,9},{11,10},{12... | collective-permute-start | bytes 98312 | tf_op jit(solution)/shard_map/ppermute | solution.py:23
  9.1 7.1 %collective-permute-start.3 = (f32[2,4,1,1024]{3,2,1,0:T(1,128)S(1)}, f32[2,4,1,1024]{3,2,1,0:T(1,128)S(1)}, u32[]{:S(2)}, u32[]{:S(2)}) collective-permute-start(f32[2,4,1,1024]{3,2,1,0:T(1,128)S(1)} %get-tuple-element.23), channel_id=1, source_target_pairs={{0,1},{1,2},{2,3},{3,4},{4,5},{5,6},{6,7},{8,9},{9,10},{10,11},{11... | collective-permute-start | bytes 98312 | tf_op jit(solution)/shard_map/ppermute | solution.py:22
  16.9 16.4 %collective-permute-start.4 = (f32[2,1,16,1024]{3,2,1,0:T(8,128)S(1)}, f32[2,1,16,1024]{3,2,1,0:T(8,128)S(1)}, u32[]{:S(2)}, u32[]{:S(2)}) collective-permute-start(f32[2,1,16,1024]{3,2,1,0:T(8,128)S(1)} %get-tuple-element.21), channel_id=1, source_target_pairs={{8,0},{16,8},{24,16},{32,24},{40,32},{48,40},{56,48},{64,56},{72,6... | collective-permute-start | bytes 393224 | tf_op jit(solution)/shard_map/ppermute | solution.py:23
  19.8 13.5 %collective-permute-start.5 = (f32[2,1,16,1024]{3,2,1,0:T(8,128)S(1)}, f32[2,1,16,1024]{3,2,1,0:T(8,128)S(1)}, u32[]{:S(2)}, u32[]{:S(2)}) collective-permute-start(f32[2,1,16,1024]{3,2,1,0:T(8,128)S(1)} %get-tuple-element.20), channel_id=1, source_target_pairs={{0,8},{8,16},{16,24},{24,32},{32,40},{40,48},{48,56},{56,64},{64,7... | collective-permute-start | bytes 393224 | tf_op jit(solution)/shard_map/ppermute | solution.py:22
  24.6 7.1 %collective-permute-start.6 = (f32[2,4,1,1024]{3,2,1,0:T(1,128)S(1)}, f32[2,4,1,1024]{3,2,1,0:T(1,128)S(1)}, u32[]{:S(2)}, u32[]{:S(2)}) collective-permute-start(f32[2,4,1,1024]{3,2,1,0:T(1,128)S(1)} %get-tuple-element.18), channel_id=1, source_target_pairs={{1,0},{2,1},{3,2},{4,3},{5,4},{6,5},{7,6},{9,8},{10,9},{11,10},{12... | collective-permute-start | bytes 98312 | tf_op jit(solution)/shard_map/ppermute | solution.py:23
  26.6 6.7 %collective-permute-start.7 = (f32[2,4,1,1024]{3,2,1,0:T(1,128)S(1)}, f32[2,4,1,1024]{3,2,1,0:T(1,128)S(1)}, u32[]{:S(2)}, u32[]{:S(2)}) collective-permute-start(f32[2,4,1,1024]{3,2,1,0:T(1,128)S(1)} %get-tuple-element.19), channel_id=1, source_target_pairs={{0,1},{1,2},{2,3},{3,4},{4,5},{5,6},{6,7},{8,9},{9,10},{10,11},{11... | collective-permute-start | bytes 98312 | tf_op jit(solution)/shard_map/ppermute | solution.py:22
  31.8 2.9 %copy-start.4 = (f32[4,16,1024]{2,1,0:T(8,128)S(1)}, f32[4,16,1024]{2,1,0:T(8,128)}, u32[]{:S(2)}) copy-start(f32[4,16,1024]{2,1,0:T(8,128)} %param.10) | copy-start | bytes 786436
  34.6 0.7 copy-start.2
  45.0 6.8 %collective-permute-start.8 = (f32[4,16,512]{2,1,0:T(8,128)S(1)}, f32[4,16,512]{2,1,0:T(8,128)S(1)}, u32[]{:S(2)}, u32[]{:S(2)}) collective-permute-start(f32[4,16,512]{2,1,0:T(8,128)S(1)} %constant_dynamic-slice_fusion), channel_id=1, source_target_pairs={{0,8},{8,0},{16,24},{24,16},{32,40},{40,32},{48,56},{56,48},{64,72... | collective-permute-start | bytes 393224 | tf_op jit(solution)/shard_map/ppermute | solution.py:37
  51.9 6.3 %collective-permute-start.9 = (f32[4,16,256]{2,1,0:T(8,128)S(1)}, f32[4,16,256]{2,1,0:T(8,128)S(1)}, u32[]{:S(2)}, u32[]{:S(2)}) collective-permute-start(f32[4,16,256]{2,1,0:T(8,128)S(1)} %fusion.50), channel_id=1, source_target_pairs={{0,16},{8,24},{16,0},{24,8},{32,48},{40,56},{48,32},{56,40},{64,80... | collective-permute-start | bytes 196616 | tf_op jit(solution)/shard_map/ppermute | solution.py:37
  58.3 7.3 %collective-permute-start.10 = (f32[4,16,128]{2,1,0:T(8,128)S(1)}, f32[4,16,128]{2,1,0:T(8,128)S(1)}, u32[]{:S(2)}, u32[]{:S(2)}) collective-permute-start(f32[4,16,128]{2,1,0:T(8,128)S(1)} %fusion.65), channel_id=1, source_target_pairs={{0,32},{8,40},{16,48},{24,56},{32,0},{40,8},{48,16},{56,24},{64,96... | collective-permute-start | bytes 98312 | tf_op jit(solution)/shard_map/ppermute | solution.py:37
  65.7 5.8 %collective-permute-start.11 = (f32[4,16,64]{2,1,0:T(8,128)S(1)}, f32[4,16,64]{2,1,0:T(8,128)S(1)}, u32[]{:S(2)}, u32[]{:S(2)}) collective-permute-start(f32[4,16,64]{2,1,0:T(8,128)S(1)} %fusion.63), channel_id=1, source_target_pairs={{0,64},{8,72},{16,80},{24,88},{32,96},{40,104},{48,112},{56,120},{... | collective-permute-start | bytes 49160 | tf_op jit(solution)/shard_map/ppermute | solution.py:37
  71.7 6.7 %collective-permute-start.12 = (f32[4,16,32]{2,1,0:T(8,128)S(1)}, f32[4,16,32]{2,1,0:T(8,128)S(1)}, u32[]{:S(2)}, u32[]{:S(2)}) collective-permute-start(f32[4,16,32]{2,1,0:T(8,128)S(1)} %fusion.61), channel_id=1, source_target_pairs={{0,128},{8,136},{16,144},{24,152},{32,160},{40,168},{48,176},{56,1... | collective-permute-start | bytes 24584 | tf_op jit(solution)/shard_map/ppermute | solution.py:37
  78.6 10.1 %collective-permute-start.13 = (f32[4,16,16]{2,1,0:T(8,128)S(1)}, f32[4,16,16]{2,1,0:T(8,128)S(1)}, u32[]{:S(2)}, u32[]{:S(2)}) collective-permute-start(f32[4,16,16]{2,1,0:T(8,128)S(1)} %fusion.59), channel_id=1, source_target_pairs={{0,256},{8,264},{16,272},{24,280},{32,288},{40,296},{48,304},{56,3... | collective-permute-start | bytes 12296 | tf_op jit(solution)/shard_map/ppermute | solution.py:37
where the time goes:
time: 89.9 us; the launch traced here: 89.4 us
  starting transfers between devices  41.9 us (47%)
  waiting for transfers between devices  29.2 us (32%)
  other arithmetic  9.12 us (10%)
  local copies, waits for them, and re-layouts  7.95 us (9%)
  between operations  1.22 us (1%)
    ppermute x6, waiting for transfers between devices, swapped(): return lax.ppermute(value, axis, pairs)  27.4 us
    ppermute x4, starting transfers between devices, extended(): lax.ppermute(last, axis, up)  17.6 us
    ppermute x6, starting transfers between devices, swapped(): return lax.ppermute(value, axis, pairs)  15.4 us
    ppermute x4, starting transfers between devices, extended(): lax.ppermute(first, axis, [(b, a) for a, b in up])  8.89 us
    another operation x3, other arithmetic, body(): fields = jnp.stack([substrate, catalyst])  3.25 us
    reshape x1, local copies, waits for them, and re-layouts, body(): jnp.transpose(shaped, order).reshape((4, row_cells, columns))  3.15 us
    another operation x4, local copies, waits for them, and re-layouts, body(): jnp.stack([jnp.sum(weights * colors[0], axis=0), jnp.sum(weights * colors...  2.83 us
    transpose x1, local copies, waits for them, and re-layouts, body(): jnp.transpose(shaped, order).reshape((4, row_cells, columns))  1.91 us
  transfers between devices with their start and end apart: 14, of which 8 were waited for; matrix products, arithmetic and copies ran while one was open for 3% of the time, Pallas kernels for 0%

commit v1 on v0

v1 whole, which is shorter than its diff:
```python
import jax
import jax.numpy as jnp
from jax import lax
from jax.experimental import pallas as pl
from jax.experimental.pallas import tpu as pltpu
from jax.sharding import PartitionSpec as P

MESH = pl.DeviceIdType.MESH
X, Y = 4, 8
CHIPS = X * Y
DEPTHS = 2 * CHIPS
ZS = 8
CT = 8
LAYERS = 4
TILE = 32
COEF = (0.16, 0.08)
FIRST = 8


def expand(tile, lane):
    light = jnp.where(lane >= 96, tile, 0.0)
    light = light + pltpu.roll(light, 32, 1)
    return light + pltpu.roll(light, 64, 1)


def regroup(tiles, lane):
    tiles = list(tiles)
    for bit in (1, 2, 4):
        low_half = (lane & (16 * bit)) == 0
        for g in range(8):
            if g & bit:
                continue
            low, high = tiles[g], tiles[g | bit]
            tiles[g] = jnp.where(low_half, low, pltpu.roll(high, 16 * bit, 1))
            tiles[g | bit] = jnp.where(low_half, pltpu.roll(low, 128 - 16 * bit, 1), high)
    return tiles


def kernel(pal, S, C, F, K, E, out_s, out_c, img,
           s0, s1, fv, kv, ev, h0, ph, ps, r0, r1, rs0, rs1, dg, new, mid, t0, cr, x0, xr,
           load_sem, out_sem, h_send, h_recv, p_send, p_recv, r0_send, r0_recv, r1_send, r1_recv,
           g_send, g_recv, c_send, c_recv, x_send, x_recv, chain):
    d = lax.axis_index("depth")
    z = lax.axis_index("rows")
    core = d % 2
    x = (d // 2) % X
    y = d // (2 * X)
    chip = d // 2

    def at(yy, xx, cc):
        return (yy * X + xx) * 2 + cc

    has = {"lo": d > 0, "hi": d < DEPTHS - 1, "zlo": z > 0, "zhi": z < ZS - 1}
    up, down = jnp.minimum(d + 1, DEPTHS - 1), jnp.maximum(d - 1, 0)
    zup, zdown = jnp.minimum(z + 1, ZS - 1), jnp.maximum(z - 1, 0)
    x_ring = (at(y, (x + 1) % X, core), at(y, (x + X - 1) % X, core))
    y_ring = (at((y + 1) % Y, x, core), at((y + Y - 1) % Y, x, core))

    for ct in range(CT):
        for sp, src in ((0, S), (1, C)):
            pltpu.make_async_copy(
                src.at[:, :, pl.ds(ct * 128, 128)],
                s0.at[sp, :, pl.ds((ct + 1) * TILE + FIRST, 16), :],
                load_sem.at[sp],
            ).start()
    f_load = pltpu.make_async_copy(F, fv, load_sem.at[2])
    k_load = pltpu.make_async_copy(K, kv, load_sem.at[3])
    e_load = pltpu.make_async_copy(E, ev, load_sem.at[4])
    f_load.start()
    k_load.start()
    e_load.start()

    barrier = pltpu.get_barrier_semaphore()

    def signal(sem, depth, row):
        pl.semaphore_signal(sem, inc=1, device_id=(depth, row), device_id_type=MESH)

    for flag, depth, row in (("lo", down, z), ("hi", up, z), ("zlo", d, zdown), ("zhi", d, zup)):
        @pl.when(has[flag])
        def _(depth=depth, row=row):
            signal(barrier, depth, row)
    for depth in x_ring + y_ring:
        signal(barrier, depth, z)

    zero = jnp.zeros((8, 128), jnp.float32)
    for sp in range(2):
        for layer in range(LAYERS):
            for buf in (s0, s1):
                for t in (0, CT + 1):
                    for rb in range(2):
                        buf[sp, layer, pl.ds(t * TILE + FIRST + 8 * rb, 8), :] = zero
            for row in (FIRST - 1, FIRST + 16):
                s0[sp, layer, pl.ds(TILE + row, CT, stride=TILE), :] = zero
    for side, flag in ((0, "lo"), (1, "hi")):
        @pl.when(jnp.logical_not(has[flag]))
        def _(side=side):
            for sp in range(2):
                for rowside in range(2):
                    dg[side, rowside, sp] = zero

                def fill(i, carry):
                    h0[side, sp, :, pl.ds(i * 128, 128)] = jnp.zeros((16, 128), jnp.float32)
                    ph[side, sp, pl.ds(i * 16, 16), :] = jnp.zeros((16, 128), jnp.float32)
                    return carry

                lax.fori_loop(0, CT, fill, 0)
    for side, flag in ((0, "zlo"), (1, "zhi")):
        @pl.when(jnp.logical_not(has[flag]))
        def _(side=side):
            for sp in range(2):
                for layer in range(LAYERS):
                    r0[side, sp, layer] = zero
                    r1[side, sp, layer] = zero

    neighbours = 4 + sum(jnp.where(has[flag], 1, 0) for flag in has)
    pl.semaphore_wait(barrier, neighbours)

    def remote(src, dst, send, recv, depth, row):
        return pltpu.make_async_remote_copy(
            src_ref=src, dst_ref=dst, send_sem=send, recv_sem=recv,
            device_id=(depth, row), device_id_type=MESH)

    def depth_copy(kind, side, sp):
        target = up if side == 0 else down
        if kind == "h":
            src = (S, C)[sp].at[LAYERS - 1 if side == 0 else 0]
            return remote(src, h0.at[side, sp], h_send.at[side, sp], h_recv.at[side, sp], target, z)
        if kind == "p":
            return remote(ps.at[side, sp], ph.at[side, sp], p_send.at[side, sp], p_recv.at[side, sp], target, z)
        rowside = int(kind)
        return remote(r0.at[rowside, sp, LAYERS - 1 if side == 0 else 0], dg.at[side, rowside, sp],
                      g_send.at[side, rowside, sp], g_recv.at[side, rowside, sp], target, z)

    def row_copy(kind, side, sp):
        target = zup if side == 0 else zdown
        if kind == "0":
            return remote(rs0.at[side, sp], r0.at[side, sp], r0_send.at[side, sp], r0_recv.at[side, sp], d, target)
        return remote(rs1.at[side, sp], r1.at[side, sp], r1_send.at[side, sp], r1_recv.at[side, sp], d, target)

    to = ("hi", "lo")
    source = ("lo", "hi")
    zto = ("zhi", "zlo")
    zsource = ("zlo", "zhi")

    def each(flag, copies, what):
        @pl.when(has[flag])
        def _():
            for copy in copies:
                getattr(copy, what)()

    for side in range(2):
        each(to[side], [depth_copy("h", side, sp) for sp in range(2)], "start")

    def ring_round(k, ring):
        for depth in ring:
            signal(chain.at[k], depth, z)

    ring_round(0, x_ring)

    for sp in range(2):
        whole = s0.at[sp, :, pl.ds(0, CT * 16), :]
        pltpu.make_async_copy(whole, whole, load_sem.at[sp]).wait()
    for side in range(2):
        row = TILE + FIRST + (15 if side == 0 else 0)
        for sp in range(2):
            for layer in range(LAYERS):
                rs0[side, sp, layer] = s0[sp, layer, pl.ds(row, CT, stride=TILE), :]
        each(zto[side], [row_copy("0", side, sp) for sp in range(2)], "start")

    f_load.wait()
    k_load.wait()

    lane = lax.broadcasted_iota(jnp.int32, (8, 128), 1)

    def start_of(ct, rb):
        return pl.multiple_of((ct + 1) * TILE + FIRST + 8 * rb, 8)

    def centre(buf, sp, layer, ct, rb):
        return buf[sp, layer, pl.ds(start_of(ct, rb), 8), :]

    def around(buf, sp, layer, ct, rb):
        here = centre(buf, sp, layer, ct, rb)
        left = centre(buf, sp, layer, ct - 1, rb)
        right = centre(buf, sp, layer, ct + 1, rb)
        total = pltpu.roll(jnp.where(lane == 127, left, here), 1, 1)
        total += pltpu.roll(jnp.where(lane == 0, right, here), 127, 1)
        base = start_of(ct, rb)
        total += buf[sp, layer, pl.ds(base - 1, 8), :]
        total += buf[sp, layer, pl.ds(base + 1, 8), :]
        return here, total

    def native(ref, layer, ct, rb):
        return ref[layer, pl.ds(8 * rb, 8), pl.ds(pl.multiple_of(ct * 128, 128), 128)]

    def react(s, c, around_s, around_c, layer, ct, rb):
        feed = native(fv, layer, ct, rb)
        kill = native(kv, layer, ct, rb)
        feed = feed + feed
        reaction = s * c * c
        reaction = reaction + reaction
        new_s = COEF[0] * around_s + (feed + s * (0.04 - feed)) - reaction
        new_c = COEF[1] * around_c + c * (0.52 - feed - (kill + kill)) + reaction
        return new_s, new_c

    def first(layers):
        def body(ct, carry):
            for layer in layers:
                for rb in range(2):
                    values = []
                    for sp in range(2):
                        here, total = around(s0, sp, layer, ct, rb)
                        if layer > 0:
                            total += centre(s0, sp, layer - 1, ct, rb)
                        if layer < LAYERS - 1:
                            total += centre(s0, sp, layer + 1, ct, rb)
                        values.append((here, total))
                    result = react(values[0][0], values[1][0], values[0][1], values[1][1], layer, ct, rb)
                    for sp in range(2):
                        s1[sp, layer, pl.ds(start_of(ct, rb), 8), :] = result[sp]
                        if layer == LAYERS - 1:
                            ps[0, sp, pl.ds(pl.multiple_of(ct * 16 + 8 * rb, 8), 8), :] = result[sp]
                        if layer == 0:
                            ps[1, sp, pl.ds(pl.multiple_of(ct * 16 + 8 * rb, 8), 8), :] = result[sp]
            return carry

        lax.fori_loop(0, CT, body, 0)

    first((0, LAYERS - 1))
    for side in range(2):
        each(to[side], [depth_copy("p", side, sp) for sp in range(2)], "start")
    first(range(1, LAYERS - 1))
    for side in range(2):
        row = TILE + FIRST + (15 if side == 0 else 0)
        for sp in range(2):
            for layer in range(LAYERS):
                rs1[side, sp, layer] = s1[sp, layer, pl.ds(row, CT, stride=TILE), :]
        each(zto[side], [row_copy("1", side, sp) for sp in range(2)], "start")

    pl.semaphore_wait(chain.at[0], 2)
    ring_round(1, y_ring)

    for side in range(2):
        each(zsource[side], [row_copy("0", side, sp) for sp in range(2)], "wait_recv")
    for side in range(2):
        each(to[side], [depth_copy(str(rowside), side, sp) for rowside in range(2) for sp in range(2)], "start")

    pl.semaphore_wait(chain.at[1], 2)
    ring_round(2, y_ring)

    scale = {flag: jnp.where(has[flag], 1.0, 0.0).astype(jnp.float32) for flag in has}
    for side in range(2):
        row = TILE + FIRST + (0 if side == 0 else 15)
        for sp in range(2):
            for layer in range(LAYERS):
                where = pl.ds(row, CT, stride=TILE)
                s1[sp, layer, where, :] = s1[sp, layer, where, :] + COEF[sp] * r0[side, sp, layer]
    for side in range(2):
        each(zsource[side], [row_copy("1", side, sp) for sp in range(2)], "wait_recv")
    for side in range(2):
        edge = TILE + FIRST + (0 if side == 0 else 15)
        outside = TILE + FIRST + (-1 if side == 0 else 16)
        for sp in range(2):
            factor = COEF[sp] * scale[zsource[side]]
            for layer in range(LAYERS):
                s1[sp, layer, pl.ds(outside, CT, stride=TILE), :] = (
                    r1[side, sp, layer] + factor * s0[sp, layer, pl.ds(edge, CT, stride=TILE), :])
    pl.semaphore_wait(chain.at[2], 2)
    ring_round(3, y_ring)

    for side in range(2):
        each(source[side], [depth_copy("h", side, sp) for sp in range(2)], "wait_recv")

    def add_layers(ct, carry):
        for side, layer in ((0, 0), (1, LAYERS - 1)):
            for sp in range(2):
                for rb in range(2):
                    where = pl.ds(start_of(ct, rb), 8)
                    halo = h0[side, sp, pl.ds(8 * rb, 8), pl.ds(pl.multiple_of(ct * 128, 128), 128)]
                    s1[sp, layer, where, :] = s1[sp, layer, where, :] + COEF[sp] * halo
        return carry

    lax.fori_loop(0, CT, add_layers, 0)
    pl.semaphore_wait(chain.at[3], 2)
    ring_round(4, y_ring)

    e_load.wait()
    weights = []
    for k in range(3):
        a, b = -8.0 * pal[k, 0], -8.0 * pal[k, 1]
        weights.append((a, b, -pal[k, 2] - 0.65 * a - 0.25 * b))

    def second(layer, ct, rb):
        values = []
        for sp in range(2):
            here, total = around(s1, sp, layer, ct, rb)
            rows = pl.ds(pl.multiple_of(ct * 16 + 8 * rb, 8), 8)
            if layer > 0:
                total += centre(s1, sp, layer - 1, ct, rb)
            else:
                total += ph[0, sp, rows, :] + (COEF[sp] * scale["lo"]) * centre(s0, sp, 0, ct, rb)
            if layer < LAYERS - 1:
                total += centre(s1, sp, layer + 1, ct, rb)
            else:
                total += ph[1, sp, rows, :] + (COEF[sp] * scale["hi"]) * centre(s0, sp, LAYERS - 1, ct, rb)
            values.append((here, total))
        s, c = react(values[0][0], values[1][0], values[0][1], values[1][1], layer, ct, rb)
        columns = pl.ds(pl.multiple_of(ct * 128, 128), 128)
        new[0, layer, pl.ds(8 * rb, 8), columns] = s
        new[1, layer, pl.ds(8 * rb, 8), columns] = c
        passing = jnp.exp(-native(ev, layer, ct, rb) * (0.25 + 4.0 * c * c))
        opacity = 1.0 - passing
        colors = [opacity / (1.0 + jnp.exp(a * s + b * c + e)) for a, b, e in weights]
        return colors, passing

    def middle(ct, carry):
        for rb in range(2):
            rows = pl.ds(pl.multiple_of(ct * 16 + 8 * rb, 8), 8)
            near, light = second(1, ct, rb)
            far, light_far = second(2, ct, rb)
            for k in range(3):
                mid[k, rows, :] = near[k] + light * far[k]
            mid[3, rows, :] = light * light_far
        return carry

    lax.fori_loop(0, CT, middle, 0)
    pl.semaphore_wait(chain.at[4], 2)

    for side in range(2):
        each(source[side], [depth_copy(str(rowside), side, sp) for rowside in range(2) for sp in range(2)], "wait_recv")
    for rowside in range(2):
        outside = TILE + FIRST + (-1 if rowside == 0 else 16)
        for sp in range(2):
            factor = COEF[sp] * scale[zsource[rowside]]
            for side, layer in ((0, 0), (1, LAYERS - 1)):
                where = pl.ds(outside, CT, stride=TILE)
                s1[sp, layer, where, :] = s1[sp, layer, where, :] + factor * dg[side, rowside, sp]
    for side in range(2):
        each(source[side], [depth_copy("p", side, sp) for sp in range(2)], "wait_recv")
    for rowside in range(2):
        for sp in range(2):
            for side in range(2):
                factor = COEF[sp] * scale[source[side]]
                where = pl.ds(0 if rowside == 0 else 15, CT, stride=16)
                ph[side, sp, where, :] = ph[side, sp, where, :] + factor * dg[side, rowside, sp]

    partner = d + 1 - 2 * core

    def core_copy(ct):
        some = pl.ds(ct * X, X)
        return remote(t0.at[1 - core, some], cr.at[some], c_send.at[ct], c_recv.at[ct], partner, z)

    def ends(ct, carry):
        tiles = [None] * 8
        for rb in range(2):
            rows = pl.ds(pl.multiple_of(ct * 16 + 8 * rb, 8), 8)
            near, light = second(0, ct, rb)
            far, light_far = second(LAYERS - 1, ct, rb)
            light_mid = light * mid[3, rows, :]
            for k in range(3):
                tiles[2 * k + rb] = near[k] + light * mid[k, rows, :] + light_mid * far[k]
            tiles[6 + rb] = light_mid * light_far
        for j, tile in enumerate(regroup(tiles, lane)):
            t0[j % 2, ct * X + j // 2] = tile
        core_copy(ct).start()
        return carry

    lax.fori_loop(0, CT, ends, 0)

    out_copies = [pltpu.make_async_copy(new.at[0], out_s, out_sem.at[0]),
                  pltpu.make_async_copy(new.at[1], out_c, out_sem.at[1])]
    for copy in out_copies:
        copy.start()

    def chip_copy(i):
        return remote(x0.at[i], xr.at[chip], x_send, x_recv, 2 * i + core, z)

    def merge(ct, carry):
        core_copy(ct).wait_recv()
        for xx in range(X):
            i = ct * X + xx
            mine, other = t0[core, i], cr[i]
            near = jnp.where(core == 0, mine, other)
            far = jnp.where(core == 0, other, mine)
            both = jnp.where(lane < 96, near, 0.0) + expand(near, lane) * far
            x0[i] = both

            @pl.when(i == chip)
            def _(i=i, both=both):
                xr[i] = both

            @pl.when(i != chip)
            def _(i=i):
                chip_copy(i).start()
        return carry

    lax.fori_loop(0, CT, merge, 0)
    arrived = xr.at[pl.ds(0, CHIPS - 1)]
    pltpu.make_async_copy(arrived, arrived, x_recv).wait()

    def compose(i, carry):
        total, light = carry
        tile = xr[i]
        return total + light * jnp.where(lane < 96, tile, 0.0), light * expand(tile, lane)

    total, light = lax.fori_loop(
        0, CHIPS, compose, (jnp.zeros((8, 128), jnp.float32), jnp.ones((8, 128), jnp.float32)), unroll=8)
    tile = jnp.where(lane < 96, total, 1.0 - light)
    for g in range(8):
        part = tile if g == 0 else pltpu.roll(tile, 128 - 16 * g, 1)
        img[g // 2, pl.ds(8 * (g % 2), 8), :] = part[:, :16]

    for side in range(2):
        each(to[side], [depth_copy(kind, side, sp) for kind in ("h", "p", "0", "1") for sp in range(2)], "wait_send")
        each(zto[side], [row_copy(kind, side, sp) for kind in ("0", "1") for sp in range(2)], "wait_send")
    lax.fori_loop(0, CT, lambda ct, carry: (core_copy(ct).wait_send(), carry)[1], 0)
    pltpu.make_async_copy(arrived, arrived, x_send).wait()
    for copy in out_copies:
        copy.wait()


def body(substrate, catalyst, feed_rate, kill_rate, extinction, palette):
    field = jax.ShapeDtypeStruct(substrate.shape, jnp.float32)
    any_ref = pl.BlockSpec(memory_space=pl.ANY)
    f32 = jnp.float32
    dma = pltpu.SemaphoreType.DMA
    return pl.pallas_call(
        kernel,
        out_shape=(field, field, jax.ShapeDtypeStruct((4, 16, 16), f32)),
        in_specs=[pl.BlockSpec(memory_space=pltpu.SMEM)] + [any_ref] * 5,
        out_specs=(any_ref, any_ref, pl.BlockSpec(memory_space=pltpu.VMEM)),
        scratch_shapes=[
            pltpu.VMEM((2, LAYERS, (CT + 2) * TILE, 128), f32),
            pltpu.VMEM((2, LAYERS, (CT + 2) * TILE, 128), f32),
            pltpu.VMEM((LAYERS, 16, CT * 128), f32),
            pltpu.VMEM((LAYERS, 16, CT * 128), f32),
            pltpu.VMEM((LAYERS, 16, CT * 128), f32),
            pltpu.VMEM((2, 2, 16, CT * 128), f32),
            pltpu.VMEM((2, 2, CT * 16, 128), f32),
            pltpu.VMEM((2, 2, CT * 16, 128), f32),
            pltpu.VMEM((2, 2, LAYERS, CT, 128), f32),
            pltpu.VMEM((2, 2, LAYERS, CT, 128), f32),
            pltpu.VMEM((2, 2, LAYERS, CT, 128), f32),
            pltpu.VMEM((2, 2, LAYERS, CT, 128), f32),
            pltpu.VMEM((2, 2, 2, CT, 128), f32),
            pltpu.VMEM((2, LAYERS, 16, CT * 128), f32),
            pltpu.VMEM((4, CT * 16, 128), f32),
            pltpu.VMEM((2, CHIPS, 8, 128), f32),
            pltpu.VMEM((CHIPS, 8, 128), f32),
            pltpu.VMEM((CHIPS, 8, 128), f32),
            pltpu.VMEM((CHIPS, 8, 128), f32),
            dma((5,)), dma((2,)),
            dma((2, 2)), dma((2, 2)), dma((2, 2)), dma((2, 2)),
            dma((2, 2)), dma((2, 2)), dma((2, 2)), dma((2, 2)),
            dma((2, 2, 2)), dma((2, 2, 2)),
            dma((CT,)), dma((CT,)), dma, dma,
            pltpu.SemaphoreType.REGULAR((5,)),
        ],
        compiler_params=pltpu.CompilerParams(collective_id=0, has_side_effects=True),
    )(palette, substrate, catalyst, feed_rate, kill_rate, extinction)


def solution(mesh):
    split = P("depth", "rows", None)
    return jax.shard_map(
        body,
        mesh=mesh,
        in_specs=(split,) * 5 + (P(),),
        out_specs=(split, split, P(None, "rows", "depth")),
        check_vma=False,
    )
```

time: 89.9 us -> 35.3 us (0.39)
  the two profiles are of different devices: /device:TPU:222 before, /device:TPU:184 now
where the time goes in v1:
time: 35.3 us; the launch traced here: 35 us
  Pallas kernels  31.3 us (89%)
  local copies, waits for them, and re-layouts  3.09 us (9%)
  between operations  0.65 us (2%)
    pallas_call x1, Pallas kernels, body(): pl.pallas_call(kernel, out_shape=(field, field, jax.ShapeDtypeStruct((4,...  31.3 us
    unnamed x7, local copies, waits for them, and re-layouts  3.09 us

profile of v1, /device:TPU:184, one launch (start us, length us, event | category | flops | bytes accessed | tf_op | source)
XLA Modules:
  0.0 35.0 jit_solution(11520605788258811333)
XLA Ops:
  0.6 31.3 %shard_map.85 = (f32[4,16,1024]{2,1,0:T(8,128)}, f32[4,16,1024]{2,1,0:T(8,128)}, f32[4,16,16]{2,1,0:T(8,128)}) custom-call(f32[3,3]{1,0:T(4,128)} %pal.1, f32[4,16,1024]{2,1,0:T(8,128)} %S.1, f32[4,16,1024]{2,1,0:T(8,128)} %C.1, f32[4,16,1024]{2,1,0:T(8,128)} %F.1, f32[4,16,1024]{2,1,0:T(8,128)} %K.1, f32[4,16,1024]{2,1,0:T(8,128)} %E.1), custom_call_target="tpu_custom_call" | custom-call | tf_op jit(solution)/shard_map/pallas_call | solution.py:426
  31.9 0.0 copy-start
  31.9 1.7 %copy.12 = f32[4,16,1024]{2,1,0:T(8,128)} copy(f32[4,16,1024]{2,1,0:T(8,128)} %get-tuple-element.6) | data formatting | bytes 524288
  33.7 0.0 copy-done
  33.7 0.0 copy-start.1
  33.7 0.7 %copy.13 = f32[4,16,1024]{2,1,0:T(8,128)} copy(f32[4,16,1024]{2,1,0:T(8,128)S(1)} %copy-done) | data formatting | bytes 524288
  34.4 0.1 copy-done.1
  34.4 0.6 %copy.14 = f32[4,16,16]{2,1,0:T(8,128)} copy(f32[4,16,16]{2,1,0:T(8,128)S(1)} %copy-done.1) | data formatting | bytes 8192
Async XLA Ops:
  31.9 1.7 %copy-start = (f32[4,16,1024]{2,1,0:T(8,128)S(1)}, f32[4,16,1024]{2,1,0:T(8,128)}, u32[]{:S(2)}) copy-start(f32[4,16,1024]{2,1,0:T(8,128)} %get-tuple-element.7) | copy-start | bytes 786436
  33.7 0.8 %copy-start.1 = (f32[4,16,16]{2,1,0:T(8,128)S(1)}, f32[4,16,16]{2,1,0:T(8,128)}, u32[]{:S(2)}) copy-start(f32[4,16,16]{2,1,0:T(8,128)} %get-tuple-element.8) | copy-start | bytes 12292

commit v2 on v1

--- a/solution.py
+++ b/solution.py
@@ -1,3 +1,5 @@
+import contextlib
+
 import jax
 import jax.numpy as jnp
 from jax import lax
@@ -5,6 +7,7 @@
 from jax.experimental.pallas import tpu as pltpu
 from jax.sharding import PartitionSpec as P
 
+mark = contextlib.nullcontext
 MESH = pl.DeviceIdType.MESH
 X, Y = 4, 8
 CHIPS = X * Y
@@ -15,12 +18,13 @@
 TILE = 32
 COEF = (0.16, 0.08)
 FIRST = 8
+GROUP = 4
+HALF = GROUP * X
 
 
 def expand(tile, lane):
     light = jnp.where(lane >= 96, tile, 0.0)
-    light = light + pltpu.roll(light, 32, 1)
-    return light + pltpu.roll(light, 64, 1)
+    return light + pltpu.roll(light, 32, 1) + (pltpu.roll(light, 64, 1) + pltpu.roll(light, 96, 1))
 
 
 def regroup(tiles, lane):
@@ -36,16 +40,16 @@
     return tiles
 
 
-def kernel(pal, S, C, F, K, E, out_s, out_c, img,
-           s0, s1, fv, kv, ev, h0, ph, ps, r0, r1, rs0, rs1, dg, new, mid, t0, cr, x0, xr,
-           load_sem, out_sem, h_send, h_recv, p_send, p_recv, r0_send, r0_recv, r1_send, r1_recv,
+def kernel(palette, S, C, F, K, E, new, xr,
+           s0, s1, fv, kv, ev, h0, ph, ps, r0, r1, rs0, rs1, dg, mid, flat, t0, cr, x0, pal,
+           load_sem, h_send, h_recv, p_send, p_recv, r0_send, r0_recv, r1_send, r1_recv,
            g_send, g_recv, c_send, c_recv, x_send, x_recv, chain):
     d = lax.axis_index("depth")
     z = lax.axis_index("rows")
-    core = d % 2
-    x = (d // 2) % X
-    y = d // (2 * X)
-    chip = d // 2
+    core = d & 1
+    chip = d >> 1
+    x = chip & (X - 1)
+    y = chip >> 2
 
     def at(yy, xx, cc):
         return (yy * X + xx) * 2 + cc
@@ -53,8 +57,20 @@
     has = {"lo": d > 0, "hi": d < DEPTHS - 1, "zlo": z > 0, "zhi": z < ZS - 1}
     up, down = jnp.minimum(d + 1, DEPTHS - 1), jnp.maximum(d - 1, 0)
     zup, zdown = jnp.minimum(z + 1, ZS - 1), jnp.maximum(z - 1, 0)
-    x_ring = (at(y, (x + 1) % X, core), at(y, (x + X - 1) % X, core))
-    y_ring = (at((y + 1) % Y, x, core), at((y + Y - 1) % Y, x, core))
+    x_ring = (at(y, (x + 1) & (X - 1), core), at(y, (x + X - 1) & (X - 1), core))
+    y_ring = (at((y + 1) & (Y - 1), x, core), at((y + Y - 1) & (Y - 1), x, core))
+
+    barrier = pltpu.get_barrier_semaphore()
+
+    def signal(sem, depth, row):
+        pl.semaphore_signal(sem, inc=1, device_id=(depth, row), device_id_type=MESH)
+
+    for flag, depth, row in (("lo", down, z), ("hi", up, z), ("zlo", d, zdown), ("zhi", d, zup)):
+        @pl.when(has[flag])
+        def _(depth=depth, row=row):
+            signal(barrier, depth, row)
+    for depth in x_ring + y_ring:
+        signal(barrier, depth, z)
 
     for ct in range(CT):
         for sp, src in ((0, S), (1, C)):
@@ -63,24 +79,14 @@
                 s0.at[sp, :, pl.ds((ct + 1) * TILE + FIRST, 16), :],
                 load_sem.at[sp],
             ).start()
+    pal_load = pltpu.make_async_copy(palette, pal, load_sem.at[5])
     f_load = pltpu.make_async_copy(F, fv, load_sem.at[2])
     k_load = pltpu.make_async_copy(K, kv, load_sem.at[3])
     e_load = pltpu.make_async_copy(E, ev, load_sem.at[4])
     f_load.start()
     k_load.start()
     e_load.start()
-
-    barrier = pltpu.get_barrier_semaphore()
-
-    def signal(sem, depth, row):
-        pl.semaphore_signal(sem, inc=1, device_id=(depth, row), device_id_type=MESH)
-
-    for flag, depth, row in (("lo", down, z), ("hi", up, z), ("zlo", d, zdown), ("zhi", d, zup)):
-        @pl.when(has[flag])
-        def _(depth=depth, row=row):
-            signal(barrier, depth, row)
-    for depth in x_ring + y_ring:
-        signal(barrier, depth, z)
+    pal_load.start()
 
     zero = jnp.zeros((8, 128), jnp.float32)
     for sp in range(2):
@@ -113,7 +119,8 @@
                     r1[side, sp, layer] = zero
 
     neighbours = 4 + sum(jnp.where(has[flag], 1, 0) for flag in has)
-    pl.semaphore_wait(barrier, neighbours)
+    with mark("w_barrier"):
+        pl.semaphore_wait(barrier, neighbours)
 
     def remote(src, dst, send, recv, depth, row):
         return pltpu.make_async_remote_copy(
@@ -157,9 +164,10 @@
 
     ring_round(0, x_ring)
 
-    for sp in range(2):
-        whole = s0.at[sp, :, pl.ds(0, CT * 16), :]
-        pltpu.make_async_copy(whole, whole, load_sem.at[sp]).wait()
+    with mark("w_load"):
+        for sp in range(2):
+            whole = s0.at[sp, :, pl.ds(0, CT * 16), :]
+            pltpu.make_async_copy(whole, whole, load_sem.at[sp]).wait()
     for side in range(2):
         row = TILE + FIRST + (15 if side == 0 else 0)
         for sp in range(2):
@@ -167,10 +175,19 @@
                 rs0[side, sp, layer] = s0[sp, layer, pl.ds(row, CT, stride=TILE), :]
         each(zto[side], [row_copy("0", side, sp) for sp in range(2)], "start")
 
-    f_load.wait()
-    k_load.wait()
+    with mark("w_loadfk"):
+        f_load.wait()
+        k_load.wait()
 
     lane = lax.broadcasted_iota(jnp.int32, (8, 128), 1)
+
+    def in_groups(step):
+        def group(g, carry):
+            for q in range(GROUP):
+                step(g * GROUP + q, carry)
+            return carry
+
+        lax.fori_loop(0, CT // GROUP, group, 0)
 
     def start_of(ct, rb):
         return pl.multiple_of((ct + 1) * TILE + FIRST + 8 * rb, 8)
@@ -223,12 +240,17 @@
                             ps[1, sp, pl.ds(pl.multiple_of(ct * 16 + 8 * rb, 8), 8), :] = result[sp]
             return carry
 
-        lax.fori_loop(0, CT, body, 0)
-
-    first((0, LAYERS - 1))
+        in_groups(body)
+
+    with mark("first03"):
+        first((0, LAYERS - 1))
     for side in range(2):
         each(to[side], [depth_copy("p", side, sp) for sp in range(2)], "start")
-    first(range(1, LAYERS - 1))
+    with mark("w_chain0"):
+        pl.semaphore_wait(chain.at[0], 2)
+    ring_round(1, y_ring)
+    with mark("first12"):
+        first(range(1, LAYERS - 1))
     for side in range(2):
         row = TILE + FIRST + (15 if side == 0 else 0)
         for sp in range(2):
@@ -236,17 +258,20 @@
                 rs1[side, sp, layer] = s1[sp, layer, pl.ds(row, CT, stride=TILE), :]
         each(zto[side], [row_copy("1", side, sp) for sp in range(2)], "start")
 
-    pl.semaphore_wait(chain.at[0], 2)
-    ring_round(1, y_ring)
-
-    for side in range(2):
-        each(zsource[side], [row_copy("0", side, sp) for sp in range(2)], "wait_recv")
+
+    with mark("w_chain1"):
+        pl.semaphore_wait(chain.at[1], 2)
+    ring_round(2, y_ring)
+    with mark("w_row0"):
+        for side in range(2):
+            each(zsource[side], [row_copy("0", side, sp) for sp in range(2)], "wait_recv")
     for side in range(2):
         each(to[side], [depth_copy(str(rowside), side, sp) for rowside in range(2) for sp in range(2)], "start")
 
-    pl.semaphore_wait(chain.at[1], 2)
-    ring_round(2, y_ring)
-
+
+    with mark("w_chain2"):
+        pl.semaphore_wait(chain.at[2], 2)
+    ring_round(3, y_ring)
     scale = {flag: jnp.where(has[flag], 1.0, 0.0).astype(jnp.float32) for flag in has}
     for side in range(2):
         row = TILE + FIRST + (0 if side == 0 else 15)
@@ -254,8 +279,9 @@
             for layer in range(LAYERS):
                 where = pl.ds(row, CT, stride=TILE)
                 s1[sp, layer, where, :] = s1[sp, layer, where, :] + COEF[sp] * r0[side, sp, layer]
-    for side in range(2):
-        each(zsource[side], [row_copy("1", side, sp) for sp in range(2)], "wait_recv")
+    with mark("w_row1"):
+        for side in range(2):
+            each(zsource[side], [row_copy("1", side, sp) for sp in range(2)], "wait_recv")
     for side in range(2):
         edge = TILE + FIRST + (0 if side == 0 else 15)
         outside = TILE + FIRST + (-1 if side == 0 else 16)
@@ -264,11 +290,10 @@
             for layer in range(LAYERS):
                 s1[sp, layer, pl.ds(outside, CT, stride=TILE), :] = (
                     r1[side, sp, layer] + factor * s0[sp, layer, pl.ds(edge, CT, stride=TILE), :])
-    pl.semaphore_wait(chain.at[2], 2)
-    ring_round(3, y_ring)
-
-    for side in range(2):
-        each(source[side], [depth_copy("h", side, sp) for sp in range(2)], "wait_recv")
+
+    with mark("w_h"):
+        for side in range(2):
+            each(source[side], [depth_copy("h", side, sp) for sp in range(2)], "wait_recv")
 
     def add_layers(ct, carry):
         for side, layer in ((0, 0), (1, LAYERS - 1)):
@@ -279,11 +304,14 @@
                     s1[sp, layer, where, :] = s1[sp, layer, where, :] + COEF[sp] * halo
         return carry
 
-    lax.fori_loop(0, CT, add_layers, 0)
-    pl.semaphore_wait(chain.at[3], 2)
+    with mark("w_chain3"):
+        pl.semaphore_wait(chain.at[3], 2)
     ring_round(4, y_ring)
+    with mark("addlayers"):
+        in_groups(add_layers)
 
     e_load.wait()
+    pal_load.wait()
     weights = []
     for k in range(3):
         a, b = -8.0 * pal[k, 0], -8.0 * pal[k, 1]
@@ -322,11 +350,12 @@
             mid[3, rows, :] = light * light_far
         return carry
 
-    lax.fori_loop(0, CT, middle, 0)
-    pl.semaphore_wait(chain.at[4], 2)
-
-    for side in range(2):
-        each(source[side], [depth_copy(str(rowside), side, sp) for rowside in range(2) for sp in range(2)], "wait_recv")
+    with mark("middle"):
+        in_groups(middle)
+
+    with mark("w_diag"):
+        for side in range(2):
+            each(source[side], [depth_copy(str(rowside), side, sp) for rowside in range(2) for sp in range(2)], "wait_recv")
     for rowside in range(2):
         outside = TILE + FIRST + (-1 if rowside == 0 else 16)
         for sp in range(2):
@@ -334,8 +363,9 @@
             for side, layer in ((0, 0), (1, LAYERS - 1)):
                 where = pl.ds(outside, CT, stride=TILE)
                 s1[sp, layer, where, :] = s1[sp, layer, where, :] + factor * dg[side, rowside, sp]
-    for side in range(2):
-        each(source[side], [depth_copy("p", side, sp) for sp in range(2)], "wait_recv")
+    with mark("w_p"):
+        for side in range(2):
+            each(source[side], [depth_copy("p", side, sp) for sp in range(2)], "wait_recv")
     for rowside in range(2):
         for sp in range(2):
             for side in range(2):
@@ -345,76 +375,83 @@
 
     partner = d + 1 - 2 * core
 
-    def core_copy(ct):
-        some = pl.ds(ct * X, X)
-        return remote(t0.at[1 - core, some], cr.at[some], c_send.at[ct], c_recv.at[ct], partner, z)
-
-    def ends(ct, carry):
-        tiles = [None] * 8
-        for rb in range(2):
-            rows = pl.ds(pl.multiple_of(ct * 16 + 8 * rb, 8), 8)
-            near, light = second(0, ct, rb)
-            far, light_far = second(LAYERS - 1, ct, rb)
-            light_mid = light * mid[3, rows, :]
-            for k in range(3):
-                tiles[2 * k + rb] = near[k] + light * mid[k, rows, :] + light_mid * far[k]
-            tiles[6 + rb] = light_mid * light_far
-        for j, tile in enumerate(regroup(tiles, lane)):
-            t0[j % 2, ct * X + j // 2] = tile
-        core_copy(ct).start()
+    def core_copy(g):
+        some = pl.ds(g * HALF, HALF)
+        return remote(t0.at[1 - core, some], cr.at[some], c_send.at[g], c_recv.at[g], partner, z)
+
+    def ends(g, carry):
+        for q in range(GROUP):
+            ct = g * GROUP + q
+            for rb in range(2):
+                rows = pl.ds(pl.multiple_of(ct * 16 + 8 * rb, 8), 8)
+                near, light = second(0, ct, rb)
+                far, light_far = second(LAYERS - 1, ct, rb)
+                light_mid = light * mid[3, rows, :]
+                for k in range(3):
+                    flat[ct * 8 + 2 * k + rb] = near[k] + light * mid[k, rows, :] + light_mid * far[k]
+                flat[ct * 8 + 6 + rb] = light_mid * light_far
+        for q in range(GROUP):
+            ct = g * GROUP + q
+            for j, tile in enumerate(regroup([flat[ct * 8 + i] for i in range(8)], lane)):
+                t0[j % 2, ct * X + j // 2] = tile
+        core_copy(g).start()
         return carry
 
-    lax.fori_loop(0, CT, ends, 0)
-
-    out_copies = [pltpu.make_async_copy(new.at[0], out_s, out_sem.at[0]),
-                  pltpu.make_async_copy(new.at[1], out_c, out_sem.at[1])]
-    for copy in out_copies:
-        copy.start()
+    with mark("ends"):
+        lax.fori_loop(0, CT // GROUP, ends, 0)
 
     def chip_copy(i):
         return remote(x0.at[i], xr.at[chip], x_send, x_recv, 2 * i + core, z)
 
-    def merge(ct, carry):
-        core_copy(ct).wait_recv()
-        for xx in range(X):
-            i = ct * X + xx
+    def merge(g, carry):
+        core_copy(g).wait_recv()
+        for q in range(HALF):
+            i = g * HALF + q
             mine, other = t0[core, i], cr[i]
             near = jnp.where(core == 0, mine, other)
             far = jnp.where(core == 0, other, mine)
-            both = jnp.where(lane < 96, near, 0.0) + expand(near, lane) * far
-            x0[i] = both
-
-            @pl.when(i == chip)
-            def _(i=i, both=both):
-                xr[i] = both
+            x0[i] = jnp.where(lane < 96, near, 0.0) + expand(near, lane) * far
+        for q in range(HALF):
+            i = g * HALF + q
 
             @pl.when(i != chip)
             def _(i=i):
                 chip_copy(i).start()
         return carry
 
-    lax.fori_loop(0, CT, merge, 0)
+    with mark("w_chain4"):
+        pl.semaphore_wait(chain.at[4], 2)
+    with mark("merge"):
+        lax.fori_loop(0, CT // GROUP, merge, 0)
+    xr[chip] = x0[chip]
     arrived = xr.at[pl.ds(0, CHIPS - 1)]
-    pltpu.make_async_copy(arrived, arrived, x_recv).wait()
-
-    def compose(i, carry):
-        total, light = carry
+    with mark("w_xy"):
+        pltpu.make_async_copy(arrived, arrived, x_recv).wait()
+
+    for side in range(2):
+        each(to[side], [depth_copy(kind, side, sp) for kind in ("h", "p", "0", "1") for sp in range(2)], "wait_send")
+        each(zto[side], [row_copy(kind, side, sp) for kind in ("0", "1") for sp in range(2)], "wait_send")
+    for g in range(CT // GROUP):
+        core_copy(g).wait_send()
+    pltpu.make_async_copy(arrived, arrived, x_send).wait()
+
+
+def finish(new, xr, out_s, out_c, img, out_sem):
+    copies = [pltpu.make_async_copy(new.at[0], out_s, out_sem.at[0]),
+              pltpu.make_async_copy(new.at[1], out_c, out_sem.at[1])]
+    for copy in copies:
+        copy.start()
+    lane = lax.broadcasted_iota(jnp.int32, (8, 128), 1)
+    total, light = jnp.zeros((8, 128), jnp.float32), jnp.ones((8, 128), jnp.float32)
+    for i in range(CHIPS):
         tile = xr[i]
-        return total + light * jnp.where(lane < 96, tile, 0.0), light * expand(tile, lane)
-
-    total, light = lax.fori_loop(
-        0, CHIPS, compose, (jnp.zeros((8, 128), jnp.float32), jnp.ones((8, 128), jnp.float32)), unroll=8)
+        total += light * jnp.where(lane < 96, tile, 0.0)
+        light *= expand(tile, lane)
     tile = jnp.where(lane < 96, total, 1.0 - light)
     for g in range(8):
         part = tile if g == 0 else pltpu.roll(tile, 128 - 16 * g, 1)
         img[g // 2, pl.ds(8 * (g % 2), 8), :] = part[:, :16]
-
-    for side in range(2):
-        each(to[side], [depth_copy(kind, side, sp) for kind in ("h", "p", "0", "1") for sp in range(2)], "wait_send")
-        each(zto[side], [row_copy(kind, side, sp) for kind in ("0", "1") for sp in range(2)], "wait_send")
-    lax.fori_loop(0, CT, lambda ct, carry: (core_copy(ct).wait_send(), carry)[1], 0)
-    pltpu.make_async_copy(arrived, arrived, x_send).wait()
-    for copy in out_copies:
+    for copy in copies:
         copy.wait()
 
 
@@ -423,11 +460,11 @@
     any_ref = pl.BlockSpec(memory_space=pl.ANY)
     f32 = jnp.float32
     dma = pltpu.SemaphoreType.DMA
-    return pl.pallas_call(
+    new, parts = pl.pallas_call(
         kernel,
-        out_shape=(field, field, jax.ShapeDtypeStruct((4, 16, 16), f32)),
-        in_specs=[pl.BlockSpec(memory_space=pltpu.SMEM)] + [any_ref] * 5,
-        out_specs=(any_ref, any_ref, pl.BlockSpec(memory_space=pltpu.VMEM)),
+        out_shape=(pltpu.VMEM((2,) + field.shape, f32), pltpu.VMEM((CHIPS, 8, 128), f32)),
+        in_specs=[any_ref] * 6,
+        out_specs=(pl.BlockSpec(memory_space=pltpu.VMEM),) * 2,
         scratch_shapes=[
             pltpu.VMEM((2, LAYERS, (CT + 2) * TILE, 128), f32),
             pltpu.VMEM((2, LAYERS, (CT + 2) * TILE, 128), f32),
@@ -442,21 +479,28 @@
             pltpu.VMEM((2, 2, LAYERS, CT, 128), f32),
             pltpu.VMEM((2, 2, LAYERS, CT, 128), f32),
             pltpu.VMEM((2, 2, 2, CT, 128), f32),
-            pltpu.VMEM((2, LAYERS, 16, CT * 128), f32),
             pltpu.VMEM((4, CT * 16, 128), f32),
+            pltpu.VMEM((CT * 8, 8, 128), f32),
             pltpu.VMEM((2, CHIPS, 8, 128), f32),
             pltpu.VMEM((CHIPS, 8, 128), f32),
             pltpu.VMEM((CHIPS, 8, 128), f32),
-            pltpu.VMEM((CHIPS, 8, 128), f32),
-            dma((5,)), dma((2,)),
+            pltpu.SMEM((3, 3), f32),
+            dma((6,)),
             dma((2, 2)), dma((2, 2)), dma((2, 2)), dma((2, 2)),
             dma((2, 2)), dma((2, 2)), dma((2, 2)), dma((2, 2)),
             dma((2, 2, 2)), dma((2, 2, 2)),
-            dma((CT,)), dma((CT,)), dma, dma,
+            dma((CT // GROUP,)), dma((CT // GROUP,)), dma, dma,
             pltpu.SemaphoreType.REGULAR((5,)),
         ],
         compiler_params=pltpu.CompilerParams(collective_id=0, has_side_effects=True),
     )(palette, substrate, catalyst, feed_rate, kill_rate, extinction)
+    return pl.pallas_call(
+        finish,
+        out_shape=(field, field, jax.ShapeDtypeStruct((4, 16, 16), f32)),
+        in_specs=[pl.BlockSpec(memory_space=pltpu.VMEM)] * 2,
+        out_specs=(any_ref, any_ref, pl.BlockSpec(memory_space=pltpu.VMEM)),
+        scratch_shapes=[dma((2,))],
+    )(*(pltpu.with_memory_space_constraint(part, pltpu.VMEM) for part in (new, parts)))
 
 
 def solution(mesh):

time: 35.3 us -> 25.7 us (0.73)
  the two profiles are of different devices: /device:TPU:184 before, /device:TPU:128 now
where the time goes in v2:
time: 25.7 us; the launch traced here: 25.6 us
  Pallas kernels  24.9 us (97%)
  between operations  0.64 us (2%)
    pallas_call x1, Pallas kernels, body(): pl.pallas_call(kernel, out_shape=(pltpu.VMEM((2,) + field.shape, f32), pl...  23.4 us
    pallas_call x1, Pallas kernels, body(): pl.pallas_call(finish, out_shape=(field, field, jax.ShapeDtypeStruct((4,...  1.51 us

profile of v2, /device:TPU:128, one launch (start us, length us, event | category | flops | bytes accessed | tf_op | source)
XLA Modules:
  0.0 25.6 jit_solution(247226699623613888)
XLA Ops:
  0.6 23.4 %shard_map.85 = (f32[2,4,16,1024]{3,2,1,0:T(8,128)S(1)}, f32[32,8,128]{2,1,0:T(8,128)S(1)}) custom-call(f32[3,3]{1,0:T(4,128)} %palette.1, f32[4,16,1024]{2,1,0:T(8,128)} %S.1, f32[4,16,1024]{2,1,0:T(8,128)} %C.1, f32[4,16,1024]{2,1,0:T(8,128)} %F.1, f32[4,16,1024]{2,1,0:T(8,128)} %K.1, f32[4,16,1024]{2,1,0:T(8,128)} %E.1), custom_call_target="tpu_custom_call" | custom-call | tf_op jit(solution)/shard_map/pallas_call | solution.py:463
  24.1 1.5 %shard_map.86 = (f32[4,16,1024]{2,1,0:T(8,128)}, f32[4,16,1024]{2,1,0:T(8,128)}, f32[4,16,16]{2,1,0:T(8,128)}) custom-call(f32[2,4,16,1024]{3,2,1,0:T(8,128)S(1)} %get-tuple-element.5.new, f32[32,8,128]{2,1,0:T(8,128)S(1)} %get-tuple-element.6.xr), custom_call_target="tpu_custom_call" | custom-call | tf_op jit(solution)/shard_map/pallas_call | solution.py:497

commit v3 on v2

--- a/solution.py
+++ b/solution.py
@@ -19,7 +19,7 @@
 COEF = (0.16, 0.08)
 FIRST = 8
 GROUP = 4
-HALF = GROUP * X
+HALF = CT // 2
 
 
 def expand(tile, lane):
@@ -106,7 +106,7 @@
 
                 def fill(i, carry):
                     h0[side, sp, :, pl.ds(i * 128, 128)] = jnp.zeros((16, 128), jnp.float32)
-                    ph[side, sp, pl.ds(i * 16, 16), :] = jnp.zeros((16, 128), jnp.float32)
+                    ph[side, i // HALF, sp, pl.ds((i % HALF) * 16, 16), :] = jnp.zeros((16, 128), jnp.float32)
                     return carry
 
                 lax.fori_loop(0, CT, fill, 0)
@@ -133,7 +133,8 @@
             src = (S, C)[sp].at[LAYERS - 1 if side == 0 else 0]
             return remote(src, h0.at[side, sp], h_send.at[side, sp], h_recv.at[side, sp], target, z)
         if kind == "p":
-            return remote(ps.at[side, sp], ph.at[side, sp], p_send.at[side, sp], p_recv.at[side, sp], target, z)
+            half = sp
+            return remote(ps.at[side, half], ph.at[side, half], p_send.at[side, half], p_recv.at[side, half], target, z)
         rowside = int(kind)
         return remote(r0.at[rowside, sp, LAYERS - 1 if side == 0 else 0], dg.at[side, rowside, sp],
                       g_send.at[side, rowside, sp], g_recv.at[side, rowside, sp], target, z)
@@ -158,11 +159,19 @@
     for side in range(2):
         each(to[side], [depth_copy("h", side, sp) for sp in range(2)], "start")
 
-    def ring_round(k, ring):
-        for depth in ring:
+    near_by = x_ring + y_ring
+    two_off = [at((y + dy) & (Y - 1), (x + dx) & (X - 1), core)
+               for dy, dx in ((2, 0), (6, 0), (0, 2), (1, 1), (1, 3), (7, 1), (7, 3))]
+
+    def spread(k, depths):
+        for depth in depths:
             signal(chain.at[k], depth, z)
 
-    ring_round(0, x_ring)
+    def heard(k, depths):
+        with mark(f"w_chain{k}"):
+            pl.semaphore_wait(chain.at[k], len(depths))
+
+    spread(0, near_by)
 
     with mark("w_load"):
         for sp in range(2):
@@ -234,10 +243,11 @@
                     result = react(values[0][0], values[1][0], values[0][1], values[1][1], layer, ct, rb)
                     for sp in range(2):
                         s1[sp, layer, pl.ds(start_of(ct, rb), 8), :] = result[sp]
-                        if layer == LAYERS - 1:
-                            ps[0, sp, pl.ds(pl.multiple_of(ct * 16 + 8 * rb, 8), 8), :] = result[sp]
-                        if layer == 0:
-                            ps[1, sp, pl.ds(pl.multiple_of(ct * 16 + 8 * rb, 8), 8), :] = result[sp]
+                        for side, edge, target in ((0, LAYERS - 1, up), (1, 0, down)):
+                            if layer == edge:
+                                place = (ct - (target >> 3) + (Y - 2)) & (Y - 1)
+                                rows = pl.multiple_of((place & (HALF - 1)) * 16 + 8 * rb, 8)
+                                ps[side, place >> 2, sp, pl.ds(rows, 8), :] = result[sp]
             return carry
 
         in_groups(body)
@@ -245,10 +255,7 @@
     with mark("first03"):
         first((0, LAYERS - 1))
     for side in range(2):
-        each(to[side], [depth_copy("p", side, sp) for sp in range(2)], "start")
-    with mark("w_chain0"):
-        pl.semaphore_wait(chain.at[0], 2)
-    ring_round(1, y_ring)
+        each(to[side], [depth_copy("p", side, 0)], "start")
     with mark("first12"):
         first(range(1, LAYERS - 1))
     for side in range(2):
@@ -259,19 +266,18 @@
         each(zto[side], [row_copy("1", side, sp) for sp in range(2)], "start")
 
 
-    with mark("w_chain1"):
-        pl.semaphore_wait(chain.at[1], 2)
-    ring_round(2, y_ring)
+    heard(0, near_by)
+    spread(1, two_off)
+
     with mark("w_row0"):
         for side in range(2):
             each(zsource[side], [row_copy("0", side, sp) for sp in range(2)], "wait_recv")
     for side in range(2):
         each(to[side], [depth_copy(str(rowside), side, sp) for rowside in range(2) for sp in range(2)], "start")
-
-
-    with mark("w_chain2"):
-        pl.semaphore_wait(chain.at[2], 2)
-    ring_round(3, y_ring)
+    for side in range(2):
+        each(to[side], [depth_copy("p", side, 1)], "start")
+
+
     scale = {flag: jnp.where(has[flag], 1.0, 0.0).astype(jnp.float32) for flag in has}
     for side in range(2):
         row = TILE + FIRST + (0 if side == 0 else 15)
@@ -304,12 +310,11 @@
                     s1[sp, layer, where, :] = s1[sp, layer, where, :] + COEF[sp] * halo
         return carry
 
-    with mark("w_chain3"):
-        pl.semaphore_wait(chain.at[3], 2)
-    ring_round(4, y_ring)
     with mark("addlayers"):
         in_groups(add_layers)
 
+    heard(1, two_off)
+    spread(2, two_off)
     e_load.wait()
     pal_load.wait()
     weights = []
@@ -317,24 +322,27 @@
         a, b = -8.0 * pal[k, 0], -8.0 * pal[k, 1]
         weights.append((a, b, -pal[k, 2] - 0.65 * a - 0.25 * b))
 
+    def columns_of(ct):
+        return pl.ds(pl.multiple_of(ct * 128, 128), 128)
+
     def second(layer, ct, rb):
         values = []
         for sp in range(2):
             here, total = around(s1, sp, layer, ct, rb)
-            rows = pl.ds(pl.multiple_of(ct * 16 + 8 * rb, 8), 8)
             if layer > 0:
                 total += centre(s1, sp, layer - 1, ct, rb)
             else:
-                total += ph[0, sp, rows, :] + (COEF[sp] * scale["lo"]) * centre(s0, sp, 0, ct, rb)
+                total += (COEF[sp] * scale["lo"]) * centre(s0, sp, 0, ct, rb)
             if layer < LAYERS - 1:
                 total += centre(s1, sp, layer + 1, ct, rb)
             else:
-                total += ph[1, sp, rows, :] + (COEF[sp] * scale["hi"]) * centre(s0, sp, LAYERS - 1, ct, rb)
+                total += (COEF[sp] * scale["hi"]) * centre(s0, sp, LAYERS - 1, ct, rb)
             values.append((here, total))
-        s, c = react(values[0][0], values[1][0], values[0][1], values[1][1], layer, ct, rb)
-        columns = pl.ds(pl.multiple_of(ct * 128, 128), 128)
-        new[0, layer, pl.ds(8 * rb, 8), columns] = s
-        new[1, layer, pl.ds(8 * rb, 8), columns] = c
+        return react(values[0][0], values[1][0], values[0][1], values[1][1], layer, ct, rb)
+
+    def shade(s, c, layer, ct, rb):
+        new[0, layer, pl.ds(8 * rb, 8), columns_of(ct)] = s
+        new[1, layer, pl.ds(8 * rb, 8), columns_of(ct)] = c
         passing = jnp.exp(-native(ev, layer, ct, rb) * (0.25 + 4.0 * c * c))
         opacity = 1.0 - passing
         colors = [opacity / (1.0 + jnp.exp(a * s + b * c + e)) for a, b, e in weights]
@@ -343,8 +351,8 @@
     def middle(ct, carry):
         for rb in range(2):
             rows = pl.ds(pl.multiple_of(ct * 16 + 8 * rb, 8), 8)
-            near, light = second(1, ct, rb)
-            far, light_far = second(2, ct, rb)
+            near, light = shade(*second(1, ct, rb), 1, ct, rb)
+            far, light_far = shade(*second(2, ct, rb), 2, ct, rb)
             for k in range(3):
                 mid[k, rows, :] = near[k] + light * far[k]
             mid[3, rows, :] = light * light_far
@@ -353,90 +361,99 @@
     with mark("middle"):
         in_groups(middle)
 
+    def open_ends(ct, carry):
+        for layer in (0, LAYERS - 1):
+            for rb in range(2):
+                for sp, value in enumerate(second(layer, ct, rb)):
+                    new[sp, layer, pl.ds(8 * rb, 8), columns_of(ct)] = value
+        return carry
+
+    with mark("open_ends"):
+        in_groups(open_ends)
+
     with mark("w_diag"):
         for side in range(2):
             each(source[side], [depth_copy(str(rowside), side, sp) for rowside in range(2) for sp in range(2)], "wait_recv")
-    for rowside in range(2):
-        outside = TILE + FIRST + (-1 if rowside == 0 else 16)
-        for sp in range(2):
-            factor = COEF[sp] * scale[zsource[rowside]]
-            for side, layer in ((0, 0), (1, LAYERS - 1)):
-                where = pl.ds(outside, CT, stride=TILE)
-                s1[sp, layer, where, :] = s1[sp, layer, where, :] + factor * dg[side, rowside, sp]
-    with mark("w_p"):
-        for side in range(2):
-            each(source[side], [depth_copy("p", side, sp) for sp in range(2)], "wait_recv")
-    for rowside in range(2):
-        for sp in range(2):
+    corner = {}
+    for side in range(2):
+        for rowside in range(2):
+            for sp in range(2):
+                corner[side, rowside, sp] = pltpu.roll(dg[side, rowside, sp], (Y - 2 - y) & (Y - 1), 0) * (2.0 * COEF[sp])
+
+    def add_corners(half):
+        for (side, rowside, sp), rows in corner.items():
+            where = pl.ds(15 * rowside, HALF, stride=16)
+            ph[side, half, sp, where, :] = ph[side, half, sp, where, :] + rows[half * HALF:half * HALF + HALF]
+
+    partner = d + 1 - 2 * core
+
+    def core_copy(g):
+        some = pl.ds(g * HALF * X, HALF * X)
+        return remote(t0.at[1 - core, some], cr.at[some], c_send.at[g], c_recv.at[g], partner, z)
+
+    def ends(g):
+        with mark(f"w_p{g}"):
             for side in range(2):
-                factor = COEF[sp] * scale[source[side]]
-                where = pl.ds(0 if rowside == 0 else 15, CT, stride=16)
-                ph[side, sp, where, :] = ph[side, sp, where, :] + factor * dg[side, rowside, sp]
-
-    partner = d + 1 - 2 * core
-
-    def core_copy(g):
-        some = pl.ds(g * HALF, HALF)
-        return remote(t0.at[1 - core, some], cr.at[some], c_send.at[g], c_recv.at[g], partner, z)
-
-    def ends(g, carry):
-        for q in range(GROUP):
-            ct = g * GROUP + q
+                each(source[side], [depth_copy("p", side, g)], "wait_recv")
+        add_corners(g)
+        for q in range(HALF):
+            place = g * HALF + q
+            ct = (y + place + 2) & (Y - 1)
             for rb in range(2):
+                parts = []
+                for side, layer in ((0, 0), (1, LAYERS - 1)):
+                    values = [new[sp, layer, pl.ds(8 * rb, 8), columns_of(ct)]
+                              + COEF[sp] * ph[side, g, sp, pl.ds(q * 16 + 8 * rb, 8), :] for sp in range(2)]
+                    parts.append(shade(*values, layer, ct, rb))
+                (near, light), (far, light_far) = parts
                 rows = pl.ds(pl.multiple_of(ct * 16 + 8 * rb, 8), 8)
-                near, light = second(0, ct, rb)
-                far, light_far = second(LAYERS - 1, ct, rb)
                 light_mid = light * mid[3, rows, :]
                 for k in range(3):
-                    flat[ct * 8 + 2 * k + rb] = near[k] + light * mid[k, rows, :] + light_mid * far[k]
-                flat[ct * 8 + 6 + rb] = light_mid * light_far
-        for q in range(GROUP):
-            ct = g * GROUP + q
-            for j, tile in enumerate(regroup([flat[ct * 8 + i] for i in range(8)], lane)):
-                t0[j % 2, ct * X + j // 2] = tile
+                    flat[place * 8 + 2 * k + rb] = near[k] + light * mid[k, rows, :] + light_mid * far[k]
+                flat[place * 8 + 6 + rb] = light_mid * light_far
+        for place in range(g * HALF, g * HALF + HALF):
+            for j, tile in enumerate(regroup([flat[place * 8 + i] for i in range(8)], lane)):
+                t0[j % 2, place * X + j // 2] = tile
         core_copy(g).start()
-        return carry
-
-    with mark("ends"):
-        lax.fori_loop(0, CT // GROUP, ends, 0)
-
-    def chip_copy(i):
-        return remote(x0.at[i], xr.at[chip], x_send, x_recv, 2 * i + core, z)
-
-    def merge(g, carry):
+
+    for g in range(2):
+        with mark(f"ends{g}"):
+            ends(g)
+
+    def chip_copy(place, away, across):
+        xx = (x + across) & (X - 1)
+        return remote(x0.at[place * X + xx], xr.at[chip], x_send, x_recv, at((y + away) & (Y - 1), xx, core), z)
+
+    def merge(g):
         core_copy(g).wait_recv()
-        for q in range(HALF):
-            i = g * HALF + q
+        for i in range(g * HALF * X, (g + 1) * HALF * X):
             mine, other = t0[core, i], cr[i]
             near = jnp.where(core == 0, mine, other)
             far = jnp.where(core == 0, other, mine)
             x0[i] = jnp.where(lane < 96, near, 0.0) + expand(near, lane) * far
-        for q in range(HALF):
-            i = g * HALF + q
-
-            @pl.when(i != chip)
-            def _(i=i):
-                chip_copy(i).start()
-        return carry
-
-    with mark("w_chain4"):
-        pl.semaphore_wait(chain.at[4], 2)
-    with mark("merge"):
-        lax.fori_loop(0, CT // GROUP, merge, 0)
-    xr[chip] = x0[chip]
+        for away in ((4, 3, 5, 2), (6, 1, 7, 0))[g]:
+            for across in (2, 1, 3, 0):
+                if away or across:
+                    chip_copy((away - 2) % Y, away, across).start()
+
+    heard(2, two_off)
+    for g in range(2):
+        with mark(f"merge{g}"):
+            merge(g)
+    for side in range(2):
+        each(to[side], [depth_copy(kind, side, sp) for kind in ("h", "p", "0", "1") for sp in range(2)], "wait_send")
+        each(zto[side], [row_copy(kind, side, sp) for kind in ("0", "1") for sp in range(2)], "wait_send")
+    for g in range(2):
+        core_copy(g).wait_send()
+    xr[chip] = x0[(Y - 2) * X + x]
     arrived = xr.at[pl.ds(0, CHIPS - 1)]
     with mark("w_xy"):
         pltpu.make_async_copy(arrived, arrived, x_recv).wait()
 
-    for side in range(2):
-        each(to[side], [depth_copy(kind, side, sp) for kind in ("h", "p", "0", "1") for sp in range(2)], "wait_send")
-        each(zto[side], [row_copy(kind, side, sp) for kind in ("0", "1") for sp in range(2)], "wait_send")
-    for g in range(CT // GROUP):
-        core_copy(g).wait_send()
     pltpu.make_async_copy(arrived, arrived, x_send).wait()
 
 
-def finish(new, xr, out_s, out_c, img, out_sem):
+def finish(new, xr, out_s, out_c, out_image, img, out_sem):
     copies = [pltpu.make_async_copy(new.at[0], out_s, out_sem.at[0]),
               pltpu.make_async_copy(new.at[1], out_c, out_sem.at[1])]
     for copy in copies:
@@ -451,6 +468,8 @@
     for g in range(8):
         part = tile if g == 0 else pltpu.roll(tile, 128 - 16 * g, 1)
         img[g // 2, pl.ds(8 * (g % 2), 8), :] = part[:, :16]
+    copies.append(pltpu.make_async_copy(img, out_image, out_sem.at[2]))
+    copies[2].start()
     for copy in copies:
         copy.wait()
 
@@ -472,8 +491,8 @@
             pltpu.VMEM((LAYERS, 16, CT * 128), f32),
             pltpu.VMEM((LAYERS, 16, CT * 128), f32),
             pltpu.VMEM((2, 2, 16, CT * 128), f32),
-            pltpu.VMEM((2, 2, CT * 16, 128), f32),
-            pltpu.VMEM((2, 2, CT * 16, 128), f32),
+            pltpu.VMEM((2, 2, 2, HALF * 16, 128), f32),
+            pltpu.VMEM((2, 2, 2, HALF * 16, 128), f32),
             pltpu.VMEM((2, 2, LAYERS, CT, 128), f32),
             pltpu.VMEM((2, 2, LAYERS, CT, 128), f32),
             pltpu.VMEM((2, 2, LAYERS, CT, 128), f32),
@@ -489,8 +508,8 @@
             dma((2, 2)), dma((2, 2)), dma((2, 2)), dma((2, 2)),
             dma((2, 2)), dma((2, 2)), dma((2, 2)), dma((2, 2)),
             dma((2, 2, 2)), dma((2, 2, 2)),
-            dma((CT // GROUP,)), dma((CT // GROUP,)), dma, dma,
-            pltpu.SemaphoreType.REGULAR((5,)),
+            dma((2,)), dma((2,)), dma, dma,
+            pltpu.SemaphoreType.REGULAR((3,)),
         ],
         compiler_params=pltpu.CompilerParams(collective_id=0, has_side_effects=True),
     )(palette, substrate, catalyst, feed_rate, kill_rate, extinction)
@@ -498,8 +517,8 @@
         finish,
         out_shape=(field, field, jax.ShapeDtypeStruct((4, 16, 16), f32)),
         in_specs=[pl.BlockSpec(memory_space=pltpu.VMEM)] * 2,
-        out_specs=(any_ref, any_ref, pl.BlockSpec(memory_space=pltpu.VMEM)),
-        scratch_shapes=[dma((2,))],
+        out_specs=(any_ref,) * 3,
+        scratch_shapes=[pltpu.VMEM((4, 16, 16), f32), dma((3,))],
     )(*(pltpu.with_memory_space_constraint(part, pltpu.VMEM) for part in (new, parts)))
 
 

time: 25.7 us -> 25.2 us (0.981)
  the two profiles are of different devices: /device:TPU:128 before, /device:TPU:192 now
where the time goes in v3:
time: 25.2 us; the launch traced here: 25.1 us
  Pallas kernels  24.4 us (97%)
  between operations  0.64 us (3%)
    pallas_call x1, Pallas kernels, body(): pl.pallas_call(kernel, out_shape=(pltpu.VMEM((2,) + field.shape, f32), pl...  23.5 us
    pallas_call x1, Pallas kernels, body(): pl.pallas_call(finish, out_shape=(field, field, jax.ShapeDtypeStruct((4,...  0.91 us

profile of v3, /device:TPU:192, one launch (start us, length us, event | category | flops | bytes accessed | tf_op | source)
XLA Modules:
  0.0 25.1 jit_solution(8184872547745457867)
XLA Ops:
  0.6 23.5 %shard_map.85 = (f32[2,4,16,1024]{3,2,1,0:T(8,128)S(1)}, f32[32,8,128]{2,1,0:T(8,128)S(1)}) custom-call(f32[3,3]{1,0:T(4,128)} %palette.1, f32[4,16,1024]{2,1,0:T(8,128)} %S.1, f32[4,16,1024]{2,1,0:T(8,128)} %C.1, f32[4,16,1024]{2,1,0:T(8,128)} %F.1, f32[4,16,1024]{2,1,0:T(8,128)} %K.1, f32[4,16,1024]{2,1,0:T(8,128)} %E.1), custom_call_target="tpu_custom_call" | custom-call | tf_op jit(solution)/shard_map/pallas_call | solution.py:482
  24.2 0.9 %shard_map.86 = (f32[4,16,1024]{2,1,0:T(8,128)}, f32[4,16,1024]{2,1,0:T(8,128)}, f32[4,16,16]{2,1,0:T(8,128)}) custom-call(f32[2,4,16,1024]{3,2,1,0:T(8,128)S(1)} %get-tuple-element.5.new, f32[32,8,128]{2,1,0:T(8,128)S(1)} %get-tuple-element.6.xr), custom_call_target="tpu_custom_call" | custom-call | tf_op jit(solution)/shard_map/pallas_call | solution.py:516

commit v4 on v3

--- a/solution.py
+++ b/solution.py
@@ -41,9 +41,9 @@
 
 
 def kernel(palette, S, C, F, K, E, new, xr,
-           s0, s1, fv, kv, ev, h0, ph, ps, r0, r1, rs0, rs1, dg, mid, flat, t0, cr, x0, pal,
+           s0, s1, fv, kv, ev, h0, ph, ps, r0, r1, rs0, rs1, eg, dg, mid, flat, t0, cr, x0, pal,
            load_sem, h_send, h_recv, p_send, p_recv, r0_send, r0_recv, r1_send, r1_recv,
-           g_send, g_recv, c_send, c_recv, x_send, x_recv, chain):
+           e_send, e_recv, g_send, g_recv, c_send, c_recv, x_send, x_recv, everyone, ready):
     d = lax.axis_index("depth")
     z = lax.axis_index("rows")
     core = d & 1
@@ -57,20 +57,23 @@
     has = {"lo": d > 0, "hi": d < DEPTHS - 1, "zlo": z > 0, "zhi": z < ZS - 1}
     up, down = jnp.minimum(d + 1, DEPTHS - 1), jnp.maximum(d - 1, 0)
     zup, zdown = jnp.minimum(z + 1, ZS - 1), jnp.maximum(z - 1, 0)
-    x_ring = (at(y, (x + 1) & (X - 1), core), at(y, (x + X - 1) & (X - 1), core))
-    y_ring = (at((y + 1) & (Y - 1), x, core), at((y + Y - 1) & (Y - 1), x, core))
 
     barrier = pltpu.get_barrier_semaphore()
 
     def signal(sem, depth, row):
         pl.semaphore_signal(sem, inc=1, device_id=(depth, row), device_id_type=MESH)
 
-    for flag, depth, row in (("lo", down, z), ("hi", up, z), ("zlo", d, zdown), ("zhi", d, zup)):
+    for flag, depth, row in (("lo", down, z), ("hi", up, z), ("zhi", d, zup)):
         @pl.when(has[flag])
         def _(depth=depth, row=row):
             signal(barrier, depth, row)
-    for depth in x_ring + y_ring:
-        signal(barrier, depth, z)
+
+    collector = at(Y // 2, X // 2, core)
+    collects = d == collector
+
+    @pl.when(jnp.logical_not(collects))
+    def _():
+        signal(barrier, collector, z)
 
     for ct in range(CT):
         for sp, src in ((0, S), (1, C)):
@@ -88,6 +91,21 @@
     e_load.start()
     pal_load.start()
 
+    with mark("w_barrier"):
+        pl.semaphore_wait(barrier, sum(jnp.where(has[flag], 1, 0) for flag in ("lo", "hi", "zlo")) + jnp.where(collects, CHIPS - 1, 0))
+
+    @pl.when(has["zlo"])
+    def _():
+        signal(ready, d, zdown)
+
+    @pl.when(collects)
+    def _():
+        def tell(i, carry):
+            signal(everyone, 2 * ((chip + i) & (CHIPS - 1)) + core, z)
+            return carry
+
+        lax.fori_loop(1, CHIPS, tell, 0)
+
     zero = jnp.zeros((8, 128), jnp.float32)
     for sp in range(2):
         for layer in range(LAYERS):
@@ -102,7 +120,7 @@
         def _(side=side):
             for sp in range(2):
                 for rowside in range(2):
-                    dg[side, rowside, sp] = zero
+                    eg[side, rowside, sp] = zero
 
                 def fill(i, carry):
                     h0[side, sp, :, pl.ds(i * 128, 128)] = jnp.zeros((16, 128), jnp.float32)
@@ -117,10 +135,8 @@
                 for layer in range(LAYERS):
                     r0[side, sp, layer] = zero
                     r1[side, sp, layer] = zero
-
-    neighbours = 4 + sum(jnp.where(has[flag], 1, 0) for flag in has)
-    with mark("w_barrier"):
-        pl.semaphore_wait(barrier, neighbours)
+                for depthside in range(2):
+                    dg[depthside, side, sp] = zero
 
     def remote(src, dst, send, recv, depth, row):
         return pltpu.make_async_remote_copy(
@@ -135,15 +151,16 @@
         if kind == "p":
             half = sp
             return remote(ps.at[side, half], ph.at[side, half], p_send.at[side, half], p_recv.at[side, half], target, z)
-        rowside = int(kind)
-        return remote(r0.at[rowside, sp, LAYERS - 1 if side == 0 else 0], dg.at[side, rowside, sp],
-                      g_send.at[side, rowside, sp], g_recv.at[side, rowside, sp], target, z)
-
-    def row_copy(kind, side, sp):
+        return remote(rs0.at[:, :, LAYERS - 1 if side == 0 else 0], eg.at[side],
+                      e_send.at[side], e_recv.at[side], target, z)
+
+    def row_copy(kind, side):
         target = zup if side == 0 else zdown
         if kind == "0":
-            return remote(rs0.at[side, sp], r0.at[side, sp], r0_send.at[side, sp], r0_recv.at[side, sp], d, target)
-        return remote(rs1.at[side, sp], r1.at[side, sp], r1_send.at[side, sp], r1_recv.at[side, sp], d, target)
+            return remote(rs0.at[side], r0.at[side], r0_send.at[side], r0_recv.at[side], d, target)
+        if kind == "corner":
+            return remote(eg.at[:, side], dg.at[:, side], g_send.at[side], g_recv.at[side], d, target)
+        return remote(rs1.at[side], r1.at[side], r1_send.at[side], r1_recv.at[side], d, target)
 
     to = ("hi", "lo")
     source = ("lo", "hi")
@@ -156,23 +173,6 @@
             for copy in copies:
                 getattr(copy, what)()
 
-    for side in range(2):
-        each(to[side], [depth_copy("h", side, sp) for sp in range(2)], "start")
-
-    near_by = x_ring + y_ring
-    two_off = [at((y + dy) & (Y - 1), (x + dx) & (X - 1), core)
-               for dy, dx in ((2, 0), (6, 0), (0, 2), (1, 1), (1, 3), (7, 1), (7, 3))]
-
-    def spread(k, depths):
-        for depth in depths:
-            signal(chain.at[k], depth, z)
-
-    def heard(k, depths):
-        with mark(f"w_chain{k}"):
-            pl.semaphore_wait(chain.at[k], len(depths))
-
-    spread(0, near_by)
-
     with mark("w_load"):
         for sp in range(2):
             whole = s0.at[sp, :, pl.ds(0, CT * 16), :]
@@ -182,7 +182,9 @@
         for sp in range(2):
             for layer in range(LAYERS):
                 rs0[side, sp, layer] = s0[sp, layer, pl.ds(row, CT, stride=TILE), :]
-        each(zto[side], [row_copy("0", side, sp) for sp in range(2)], "start")
+    for side in range(2):
+        each(to[side], [depth_copy("edge", side, 0)] + [depth_copy("h", side, sp) for sp in range(2)], "start")
+    each("zlo", [row_copy("0", 1)], "start")
 
     with mark("w_loadfk"):
         f_load.wait()
@@ -255,7 +257,7 @@
     with mark("first03"):
         first((0, LAYERS - 1))
     for side in range(2):
-        each(to[side], [depth_copy("p", side, 0)], "start")
+        each(to[side], [depth_copy("p", side, half) for half in range(2)], "start")
     with mark("first12"):
         first(range(1, LAYERS - 1))
     for side in range(2):
@@ -263,20 +265,23 @@
         for sp in range(2):
             for layer in range(LAYERS):
                 rs1[side, sp, layer] = s1[sp, layer, pl.ds(row, CT, stride=TILE), :]
-        each(zto[side], [row_copy("1", side, sp) for sp in range(2)], "start")
-
-
-    heard(0, near_by)
-    spread(1, two_off)
+    each("zlo", [row_copy("1", 1)], "start")
+    with mark("w_readyz"):
+        @pl.when(has["zhi"])
+        def _():
+            pl.semaphore_wait(ready, 1)
+            for kind in ("0", "1"):
+                row_copy(kind, 0).start()
+
+    with mark("w_edge"):
+        for side in range(2):
+            each(source[side], [depth_copy("edge", side, 0)], "wait_recv")
+    for side in range(2):
+        each(zto[side], [row_copy("corner", side)], "start")
 
     with mark("w_row0"):
         for side in range(2):
-            each(zsource[side], [row_copy("0", side, sp) for sp in range(2)], "wait_recv")
-    for side in range(2):
-        each(to[side], [depth_copy(str(rowside), side, sp) for rowside in range(2) for sp in range(2)], "start")
-    for side in range(2):
-        each(to[side], [depth_copy("p", side, 1)], "start")
-
+            each(zsource[side], [row_copy("0", side)], "wait_recv")
 
     scale = {flag: jnp.where(has[flag], 1.0, 0.0).astype(jnp.float32) for flag in has}
     for side in range(2):
@@ -287,7 +292,7 @@
                 s1[sp, layer, where, :] = s1[sp, layer, where, :] + COEF[sp] * r0[side, sp, layer]
     with mark("w_row1"):
         for side in range(2):
-            each(zsource[side], [row_copy("1", side, sp) for sp in range(2)], "wait_recv")
+            each(zsource[side], [row_copy("1", side)], "wait_recv")
     for side in range(2):
         edge = TILE + FIRST + (0 if side == 0 else 15)
         outside = TILE + FIRST + (-1 if side == 0 else 16)
@@ -313,8 +318,6 @@
     with mark("addlayers"):
         in_groups(add_layers)
 
-    heard(1, two_off)
-    spread(2, two_off)
     e_load.wait()
     pal_load.wait()
     weights = []
@@ -373,7 +376,7 @@
 
     with mark("w_diag"):
         for side in range(2):
-            each(source[side], [depth_copy(str(rowside), side, sp) for rowside in range(2) for sp in range(2)], "wait_recv")
+            each(zsource[side], [row_copy("corner", side)], "wait_recv")
     corner = {}
     for side in range(2):
         for rowside in range(2):
@@ -436,13 +439,17 @@
                 if away or across:
                     chip_copy((away - 2) % Y, away, across).start()
 
-    heard(2, two_off)
+    with mark("w_everyone"):
+        @pl.when(jnp.logical_not(collects))
+        def _():
+            pl.semaphore_wait(everyone, 1)
+
     for g in range(2):
         with mark(f"merge{g}"):
             merge(g)
     for side in range(2):
-        each(to[side], [depth_copy(kind, side, sp) for kind in ("h", "p", "0", "1") for sp in range(2)], "wait_send")
-        each(zto[side], [row_copy(kind, side, sp) for kind in ("0", "1") for sp in range(2)], "wait_send")
+        each(to[side], [depth_copy("edge", side, 0)] + [depth_copy(kind, side, i) for kind in ("h", "p") for i in range(2)], "wait_send")
+        each(zto[side], [row_copy(kind, side) for kind in ("0", "1", "corner")], "wait_send")
     for g in range(2):
         core_copy(g).wait_send()
     xr[chip] = x0[(Y - 2) * X + x]
@@ -459,11 +466,16 @@
     for copy in copies:
         copy.start()
     lane = lax.broadcasted_iota(jnp.int32, (8, 128), 1)
-    total, light = jnp.zeros((8, 128), jnp.float32), jnp.ones((8, 128), jnp.float32)
-    for i in range(CHIPS):
-        tile = xr[i]
-        total += light * jnp.where(lane < 96, tile, 0.0)
-        light *= expand(tile, lane)
+
+    def compose(g, carry):
+        total, light = carry
+        for i in range(HALF * X):
+            tile = xr[g * HALF * X + i]
+            total += light * jnp.where(lane < 96, tile, 0.0)
+            light *= expand(tile, lane)
+        return total, light
+
+    total, light = lax.fori_loop(0, 2, compose, (jnp.zeros((8, 128), jnp.float32), jnp.ones((8, 128), jnp.float32)))
     tile = jnp.where(lane < 96, total, 1.0 - light)
     for g in range(8):
         part = tile if g == 0 else pltpu.roll(tile, 128 - 16 * g, 1)
@@ -498,6 +510,7 @@
             pltpu.VMEM((2, 2, LAYERS, CT, 128), f32),
             pltpu.VMEM((2, 2, LAYERS, CT, 128), f32),
             pltpu.VMEM((2, 2, 2, CT, 128), f32),
+            pltpu.VMEM((2, 2, 2, CT, 128), f32),
             pltpu.VMEM((4, CT * 16, 128), f32),
             pltpu.VMEM((CT * 8, 8, 128), f32),
             pltpu.VMEM((2, CHIPS, 8, 128), f32),
@@ -506,10 +519,10 @@
             pltpu.SMEM((3, 3), f32),
             dma((6,)),
             dma((2, 2)), dma((2, 2)), dma((2, 2)), dma((2, 2)),
-            dma((2, 2)), dma((2, 2)), dma((2, 2)), dma((2, 2)),
-            dma((2, 2, 2)), dma((2, 2, 2)),
+            dma((2,)), dma((2,)), dma((2,)), dma((2,)),
+            dma((2,)), dma((2,)), dma((2,)), dma((2,)),
             dma((2,)), dma((2,)), dma, dma,
-            pltpu.SemaphoreType.REGULAR((3,)),
+            pltpu.SemaphoreType.REGULAR, pltpu.SemaphoreType.REGULAR,
         ],
         compiler_params=pltpu.CompilerParams(collective_id=0, has_side_effects=True),
     )(palette, substrate, catalyst, feed_rate, kill_rate, extinction)

time: 25.2 us -> 24.2 us (0.960)
  the two profiles are of different devices: /device:TPU:192 before, /device:TPU:1 now
where the time goes in v4:
time: 24.2 us; the launch traced here: 23.9 us
  Pallas kernels  23.2 us (96%)
  between operations  0.64 us (3%)
    pallas_call x1, Pallas kernels, body(): pl.pallas_call(kernel, out_shape=(pltpu.VMEM((2,) + field.shape, f32), pl...  22.2 us
    pallas_call x1, Pallas kernels, body(): pl.pallas_call(finish, out_shape=(field, field, jax.ShapeDtypeStruct((4,...  0.96 us

profile of v4, /device:TPU:1, one launch (start us, length us, event | category | flops | bytes accessed | tf_op | source)
XLA Modules:
  0.0 23.9 jit_solution(13027568307275341005)
XLA Ops:
  0.6 22.2 %shard_map.85 = (f32[2,4,16,1024]{3,2,1,0:T(8,128)S(1)}, f32[32,8,128]{2,1,0:T(8,128)S(1)}) custom-call(f32[3,3]{1,0:T(4,128)} %palette.1, f32[4,16,1024]{2,1,0:T(8,128)} %S.1, f32[4,16,1024]{2,1,0:T(8,128)} %C.1, f32[4,16,1024]{2,1,0:T(8,128)} %F.1, f32[4,16,1024]{2,1,0:T(8,128)} %K.1, f32[4,16,1024]{2,1,0:T(8,128)} %E.1), custom_call_target="tpu_custom_call" | custom-call | tf_op jit(solution)/shard_map/pallas_call | solution.py:494
  22.9 1.0 %shard_map.86 = (f32[4,16,1024]{2,1,0:T(8,128)}, f32[4,16,1024]{2,1,0:T(8,128)}, f32[4,16,16]{2,1,0:T(8,128)}) custom-call(f32[2,4,16,1024]{3,2,1,0:T(8,128)S(1)} %get-tuple-element.5.new, f32[32,8,128]{2,1,0:T(8,128)S(1)} %get-tuple-element.6.xr), custom_call_target="tpu_custom_call" | custom-call | tf_op jit(solution)/shard_map/pallas_call | solution.py:529

commit v5 on v4

--- a/solution.py
+++ b/solution.py
@@ -20,6 +20,9 @@
 FIRST = 8
 GROUP = 4
 HALF = CT // 2
+COLLECTORS = (1, (Y // 2) * X + X // 2)
+DIRECT = ((4, 2), (4, 1), (4, 3), (3, 2), (5, 2), (6, 2))
+TILES = CHIPS - 1 + len(DIRECT)
 
 
 def expand(tile, lane):
@@ -68,12 +71,12 @@
         def _(depth=depth, row=row):
             signal(barrier, depth, row)
 
-    collector = at(Y // 2, X // 2, core)
-    collects = d == collector
-
-    @pl.when(jnp.logical_not(collects))
-    def _():
-        signal(barrier, collector, z)
+    collector = jnp.where(z == 0, COLLECTORS[0], COLLECTORS[1])
+    collects = chip == collector
+    for c in range(2):
+        @pl.when(d != 2 * collector + c)
+        def _(c=c):
+            signal(barrier, 2 * collector + c, z)
 
     for ct in range(CT):
         for sp, src in ((0, S), (1, C)):
@@ -92,7 +95,7 @@
     pal_load.start()
 
     with mark("w_barrier"):
-        pl.semaphore_wait(barrier, sum(jnp.where(has[flag], 1, 0) for flag in ("lo", "hi", "zlo")) + jnp.where(collects, CHIPS - 1, 0))
+        pl.semaphore_wait(barrier, sum(jnp.where(has[flag], 1, 0) for flag in ("lo", "hi", "zlo")) + jnp.where(collects, DEPTHS - 1, 0))
 
     @pl.when(has["zlo"])
     def _():
@@ -147,10 +150,14 @@
         target = up if side == 0 else down
         if kind == "h":
             src = (S, C)[sp].at[LAYERS - 1 if side == 0 else 0]
-            return remote(src, h0.at[side, sp], h_send.at[side, sp], h_recv.at[side, sp], target, z)
+            return remote(src, h0.at[side, sp], h_send.at[side], h_recv.at[side], target, z)
+        if kind == "both":
+            return remote(h0.at[side], h0.at[side], h_send.at[side], h_recv.at[side], target, z)
+        if kind == "halves":
+            return remote(ps.at[side], ph.at[side], p_send.at[side], p_recv.at[side, 0], target, z)
         if kind == "p":
             half = sp
-            return remote(ps.at[side, half], ph.at[side, half], p_send.at[side, half], p_recv.at[side, half], target, z)
+            return remote(ps.at[side, half], ph.at[side, half], p_send.at[side], p_recv.at[side, half], target, z)
         return remote(rs0.at[:, :, LAYERS - 1 if side == 0 else 0], eg.at[side],
                       e_send.at[side], e_recv.at[side], target, z)
 
@@ -304,7 +311,7 @@
 
     with mark("w_h"):
         for side in range(2):
-            each(source[side], [depth_copy("h", side, sp) for sp in range(2)], "wait_recv")
+            each(source[side], [depth_copy("both", side, 0)], "wait_recv")
 
     def add_layers(ct, carry):
         for side, layer in ((0, 0), (1, LAYERS - 1)):
@@ -418,6 +425,17 @@
             for j, tile in enumerate(regroup([flat[place * 8 + i] for i in range(8)], lane)):
                 t0[j % 2, place * X + j // 2] = tile
         core_copy(g).start()
+        for away, across in DIRECT:
+            place = (away - 2) % Y
+            if place // HALF == g:
+                yy, xx = (y + away) & (Y - 1), (x + across) & (X - 1)
+                for c in range(2):
+                    remote(t0.at[c, place * X + xx], xr.at[CHIPS * (1 + core) + chip], x_send, x_recv, at(yy, xx, c), z).start()
+
+    with mark("w_everyone"):
+        @pl.when(jnp.logical_not(collects))
+        def _():
+            pl.semaphore_wait(everyone, 1)
 
     for g in range(2):
         with mark(f"ends{g}"):
@@ -426,36 +444,38 @@
     def chip_copy(place, away, across):
         xx = (x + across) & (X - 1)
         return remote(x0.at[place * X + xx], xr.at[chip], x_send, x_recv, at((y + away) & (Y - 1), xx, core), z)
+
+    def joined(near, far):
+        return jnp.where(lane < 96, near, 0.0) + expand(near, lane) * far
 
     def merge(g):
         core_copy(g).wait_recv()
         for i in range(g * HALF * X, (g + 1) * HALF * X):
             mine, other = t0[core, i], cr[i]
-            near = jnp.where(core == 0, mine, other)
-            far = jnp.where(core == 0, other, mine)
-            x0[i] = jnp.where(lane < 96, near, 0.0) + expand(near, lane) * far
+            x0[i] = joined(jnp.where(core == 0, mine, other), jnp.where(core == 0, other, mine))
         for away in ((4, 3, 5, 2), (6, 1, 7, 0))[g]:
             for across in (2, 1, 3, 0):
-                if away or across:
+                if (away or across) and (away, across) not in DIRECT:
                     chip_copy((away - 2) % Y, away, across).start()
-
-    with mark("w_everyone"):
-        @pl.when(jnp.logical_not(collects))
-        def _():
-            pl.semaphore_wait(everyone, 1)
 
     for g in range(2):
         with mark(f"merge{g}"):
             merge(g)
     for side in range(2):
-        each(to[side], [depth_copy("edge", side, 0)] + [depth_copy(kind, side, i) for kind in ("h", "p") for i in range(2)], "wait_send")
+        each(to[side], [depth_copy(kind, side, 0) for kind in ("edge", "both", "halves")], "wait_send")
         each(zto[side], [row_copy(kind, side) for kind in ("0", "1", "corner")], "wait_send")
     for g in range(2):
         core_copy(g).wait_send()
     xr[chip] = x0[(Y - 2) * X + x]
-    arrived = xr.at[pl.ds(0, CHIPS - 1)]
+    arrived = xr.at[pl.ds(0, TILES)]
     with mark("w_xy"):
         pltpu.make_async_copy(arrived, arrived, x_recv).wait()
+    both = []
+    for away, across in DIRECT:
+        i = ((y - away) & (Y - 1)) * X + ((x - across) & (X - 1))
+        both.append((i, joined(xr[CHIPS + i], xr[2 * CHIPS + i])))
+    for i, tile in both:
+        xr[i] = tile
 
     pltpu.make_async_copy(arrived, arrived, x_send).wait()
 
@@ -493,7 +513,7 @@
     dma = pltpu.SemaphoreType.DMA
     new, parts = pl.pallas_call(
         kernel,
-        out_shape=(pltpu.VMEM((2,) + field.shape, f32), pltpu.VMEM((CHIPS, 8, 128), f32)),
+        out_shape=(pltpu.VMEM((2,) + field.shape, f32), pltpu.VMEM((3 * CHIPS, 8, 128), f32)),
         in_specs=[any_ref] * 6,
         out_specs=(pl.BlockSpec(memory_space=pltpu.VMEM),) * 2,
         scratch_shapes=[
@@ -518,7 +538,7 @@
             pltpu.VMEM((CHIPS, 8, 128), f32),
             pltpu.SMEM((3, 3), f32),
             dma((6,)),
-            dma((2, 2)), dma((2, 2)), dma((2, 2)), dma((2, 2)),
+            dma((2,)), dma((2,)), dma((2,)), dma((2, 2)),
             dma((2,)), dma((2,)), dma((2,)), dma((2,)),
             dma((2,)), dma((2,)), dma((2,)), dma((2,)),
             dma((2,)), dma((2,)), dma, dma,

time: 24.2 us -> 23.6 us (0.975)
  Pallas kernels: 23.2 us -> 22.8 us
    pallas_call x1, Pallas kernels: 22.2 us -> 21.8 us  [body(): pl.pallas_call(kernel, out_shape=(pltpu.VMEM((2,) + field.shape, f32), pl...]
where the time goes in v5:
time: 23.6 us; the launch traced here: 23.4 us
  Pallas kernels  22.8 us (97%)
  between operations  0.64 us (3%)
    pallas_call x1, Pallas kernels, body(): pl.pallas_call(kernel, out_shape=(pltpu.VMEM((2,) + field.shape, f32), pl...  21.8 us
    pallas_call x1, Pallas kernels, body(): pl.pallas_call(finish, out_shape=(field, field, jax.ShapeDtypeStruct((4,...  0.96 us

profile of v5, /device:TPU:1, one launch (start us, length us, event | category | flops | bytes accessed | tf_op | source)
XLA Modules:
  0.0 23.4 jit_solution(1250561521293766926)
XLA Ops:
  0.6 21.8 %shard_map.85 = (f32[2,4,16,1024]{3,2,1,0:T(8,128)S(1)}, f32[96,8,128]{2,1,0:T(8,128)S(1)}) custom-call(f32[3,3]{1,0:T(4,128)} %palette.1, f32[4,16,1024]{2,1,0:T(8,128)} %S.1, f32[4,16,1024]{2,1,0:T(8,128)} %C.1, f32[4,16,1024]{2,1,0:T(8,128)} %F.1, f32[4,16,1024]{2,1,0:T(8,128)} %K.1, f32[4,16,1024]{2,1,0:T(8,128)} %E.1), custom_call_target="tpu_custom_call" | custom-call | tf_op jit(solution)/shard_map/pallas_call | solution.py:514
  22.5 1.0 %shard_map.86 = (f32[4,16,1024]{2,1,0:T(8,128)}, f32[4,16,1024]{2,1,0:T(8,128)}, f32[4,16,16]{2,1,0:T(8,128)}) custom-call(f32[2,4,16,1024]{3,2,1,0:T(8,128)S(1)} %get-tuple-element.5.new, f32[96,8,128]{2,1,0:T(8,128)S(1)} %get-tuple-element.6.xr), custom_call_target="tpu_custom_call" | custom-call | tf_op jit(solution)/shard_map/pallas_call | solution.py:549

commit v6 on v5

--- a/solution.py
+++ b/solution.py
@@ -20,7 +20,7 @@
 FIRST = 8
 GROUP = 4
 HALF = CT // 2
-COLLECTORS = (1, (Y // 2) * X + X // 2)
+COLLECTORS = (9, (Y // 2) * X + X // 2)
 DIRECT = ((4, 2), (4, 1), (4, 3), (3, 2), (5, 2), (6, 2))
 TILES = CHIPS - 1 + len(DIRECT)
 
@@ -28,6 +28,10 @@
 def expand(tile, lane):
     light = jnp.where(lane >= 96, tile, 0.0)
     return light + pltpu.roll(light, 32, 1) + (pltpu.roll(light, 64, 1) + pltpu.roll(light, 96, 1))
+
+
+def joined(near, far, lane):
+    return jnp.where(lane < 96, near, 0.0) + expand(near, lane) * far
 
 
 def regroup(tiles, lane):
@@ -46,7 +50,7 @@
 def kernel(palette, S, C, F, K, E, new, xr,
            s0, s1, fv, kv, ev, h0, ph, ps, r0, r1, rs0, rs1, eg, dg, mid, flat, t0, cr, x0, pal,
            load_sem, h_send, h_recv, p_send, p_recv, r0_send, r0_recv, r1_send, r1_recv,
-           e_send, e_recv, g_send, g_recv, c_send, c_recv, x_send, x_recv, everyone, ready):
+           e_send, e_recv, g_send, g_recv, s_send, s_recv, c_send, c_recv, x_send, x_recv, everyone, ready):
     d = lax.axis_index("depth")
     z = lax.axis_index("rows")
     core = d & 1
@@ -70,6 +74,14 @@
         @pl.when(has[flag])
         def _(depth=depth, row=row):
             signal(barrier, depth, row)
+
+    above, below = has["zlo"], has["zhi"]
+    for flag, depth in (("lo", down), ("hi", up)):
+        @pl.when(below & has[flag])
+        def _(depth=depth):
+            signal(barrier, depth, zup)
+    has["above_lo"], has["above_hi"] = above & has["lo"], above & has["hi"]
+    has["below_lo"], has["below_hi"] = below & has["lo"], below & has["hi"]
 
     collector = jnp.where(z == 0, COLLECTORS[0], COLLECTORS[1])
     collects = chip == collector
@@ -95,7 +107,7 @@
     pal_load.start()
 
     with mark("w_barrier"):
-        pl.semaphore_wait(barrier, sum(jnp.where(has[flag], 1, 0) for flag in ("lo", "hi", "zlo")) + jnp.where(collects, DEPTHS - 1, 0))
+        pl.semaphore_wait(barrier, sum(jnp.where(has[flag], 1, 0) for flag in ("lo", "hi", "zlo", "above_lo", "above_hi")) + jnp.where(collects, DEPTHS - 1, 0))
 
     @pl.when(has["zlo"])
     def _():
@@ -118,12 +130,17 @@
                         buf[sp, layer, pl.ds(t * TILE + FIRST + 8 * rb, 8), :] = zero
             for row in (FIRST - 1, FIRST + 16):
                 s0[sp, layer, pl.ds(TILE + row, CT, stride=TILE), :] = zero
+    clear = jnp.where(lax.broadcasted_iota(jnp.int32, (8, 128), 1) < 96, 0.0, 1.0)
+    for away in range(Y):
+        for across in range(X):
+            if (away, across) not in DIRECT:
+                xr[CHIPS + ((y - away) & (Y - 1)) * X + ((x - across) & (X - 1))] = clear
     for side, flag in ((0, "lo"), (1, "hi")):
         @pl.when(jnp.logical_not(has[flag]))
         def _(side=side):
             for sp in range(2):
-                for rowside in range(2):
-                    eg[side, rowside, sp] = zero
+                eg[side, 0, sp] = zero
+                dg[side, 1, sp] = zero
 
                 def fill(i, carry):
                     h0[side, sp, :, pl.ds(i * 128, 128)] = jnp.zeros((16, 128), jnp.float32)
@@ -158,7 +175,10 @@
         if kind == "p":
             half = sp
             return remote(ps.at[side, half], ph.at[side, half], p_send.at[side], p_recv.at[side, half], target, z)
-        return remote(rs0.at[:, :, LAYERS - 1 if side == 0 else 0], eg.at[side],
+        if kind == "straight":
+            return remote(rs0.at[1, :, LAYERS - 1 if side == 0 else 0], dg.at[side, 1],
+                          s_send.at[side], s_recv.at[side], target, zdown)
+        return remote(rs0.at[0:1, :, LAYERS - 1 if side == 0 else 0], eg.at[side],
                       e_send.at[side], e_recv.at[side], target, z)
 
     def row_copy(kind, side):
@@ -166,7 +186,7 @@
         if kind == "0":
             return remote(rs0.at[side], r0.at[side], r0_send.at[side], r0_recv.at[side], d, target)
         if kind == "corner":
-            return remote(eg.at[:, side], dg.at[:, side], g_send.at[side], g_recv.at[side], d, target)
+            return remote(eg.at[:, 0], dg.at[:, 0], g_send, g_recv, d, target)
         return remote(rs1.at[side], r1.at[side], r1_send.at[side], r1_recv.at[side], d, target)
 
     to = ("hi", "lo")
@@ -189,6 +209,8 @@
         for sp in range(2):
             for layer in range(LAYERS):
                 rs0[side, sp, layer] = s0[sp, layer, pl.ds(row, CT, stride=TILE), :]
+    for side in range(2):
+        each("above_" + to[side], [depth_copy("straight", side, 0)], "start")
     for side in range(2):
         each(to[side], [depth_copy("edge", side, 0)] + [depth_copy("h", side, sp) for sp in range(2)], "start")
     each("zlo", [row_copy("0", 1)], "start")
@@ -283,14 +305,13 @@
     with mark("w_edge"):
         for side in range(2):
             each(source[side], [depth_copy("edge", side, 0)], "wait_recv")
-    for side in range(2):
-        each(zto[side], [row_copy("corner", side)], "start")
+    each("zhi", [row_copy("corner", 0)], "start")
 
     with mark("w_row0"):
         for side in range(2):
             each(zsource[side], [row_copy("0", side)], "wait_recv")
 
-    scale = {flag: jnp.where(has[flag], 1.0, 0.0).astype(jnp.float32) for flag in has}
+    scale = {flag: jnp.where(has[flag], 1.0, 0.0).astype(jnp.float32) for flag in source + zsource}
     for side in range(2):
         row = TILE + FIRST + (0 if side == 0 else 15)
         for sp in range(2):
@@ -383,7 +404,8 @@
 
     with mark("w_diag"):
         for side in range(2):
-            each(zsource[side], [row_copy("corner", side)], "wait_recv")
+            each("below_" + source[side], [depth_copy("straight", side, 0)], "wait_recv")
+        each("zlo", [row_copy("corner", 0)], "wait_recv")
     corner = {}
     for side in range(2):
         for rowside in range(2):
@@ -430,7 +452,7 @@
             if place // HALF == g:
                 yy, xx = (y + away) & (Y - 1), (x + across) & (X - 1)
                 for c in range(2):
-                    remote(t0.at[c, place * X + xx], xr.at[CHIPS * (1 + core) + chip], x_send, x_recv, at(yy, xx, c), z).start()
+                    remote(t0.at[c, place * X + xx], xr.at[CHIPS * core + chip], x_send, x_recv, at(yy, xx, c), z).start()
 
     with mark("w_everyone"):
         @pl.when(jnp.logical_not(collects))
@@ -445,14 +467,11 @@
         xx = (x + across) & (X - 1)
         return remote(x0.at[place * X + xx], xr.at[chip], x_send, x_recv, at((y + away) & (Y - 1), xx, core), z)
 
-    def joined(near, far):
-        return jnp.where(lane < 96, near, 0.0) + expand(near, lane) * far
-
     def merge(g):
         core_copy(g).wait_recv()
         for i in range(g * HALF * X, (g + 1) * HALF * X):
             mine, other = t0[core, i], cr[i]
-            x0[i] = joined(jnp.where(core == 0, mine, other), jnp.where(core == 0, other, mine))
+            x0[i] = joined(jnp.where(core == 0, mine, other), jnp.where(core == 0, other, mine), lane)
         for away in ((4, 3, 5, 2), (6, 1, 7, 0))[g]:
             for across in (2, 1, 3, 0):
                 if (away or across) and (away, across) not in DIRECT:
@@ -463,20 +482,15 @@
             merge(g)
     for side in range(2):
         each(to[side], [depth_copy(kind, side, 0) for kind in ("edge", "both", "halves")], "wait_send")
-        each(zto[side], [row_copy(kind, side) for kind in ("0", "1", "corner")], "wait_send")
+        each("above_" + to[side], [depth_copy("straight", side, 0)], "wait_send")
+        each(zto[side], [row_copy(kind, side) for kind in ("0", "1")], "wait_send")
+    each("zhi", [row_copy("corner", 0)], "wait_send")
     for g in range(2):
         core_copy(g).wait_send()
     xr[chip] = x0[(Y - 2) * X + x]
     arrived = xr.at[pl.ds(0, TILES)]
     with mark("w_xy"):
         pltpu.make_async_copy(arrived, arrived, x_recv).wait()
-    both = []
-    for away, across in DIRECT:
-        i = ((y - away) & (Y - 1)) * X + ((x - across) & (X - 1))
-        both.append((i, joined(xr[CHIPS + i], xr[2 * CHIPS + i])))
-    for i, tile in both:
-        xr[i] = tile
-
     pltpu.make_async_copy(arrived, arrived, x_send).wait()
 
 
@@ -485,24 +499,34 @@
               pltpu.make_async_copy(new.at[1], out_c, out_sem.at[1])]
     for copy in copies:
         copy.start()
-    lane = lax.broadcasted_iota(jnp.int32, (8, 128), 1)
-
-    def compose(g, carry):
-        total, light = carry
-        for i in range(HALF * X):
-            tile = xr[g * HALF * X + i]
-            total += light * jnp.where(lane < 96, tile, 0.0)
-            light *= expand(tile, lane)
-        return total, light
-
-    total, light = lax.fori_loop(0, 2, compose, (jnp.zeros((8, 128), jnp.float32), jnp.ones((8, 128), jnp.float32)))
-    tile = jnp.where(lane < 96, total, 1.0 - light)
-    for g in range(8):
-        part = tile if g == 0 else pltpu.roll(tile, 128 - 16 * g, 1)
-        img[g // 2, pl.ds(8 * (g % 2), 8), :] = part[:, :16]
-    copies.append(pltpu.make_async_copy(img, out_image, out_sem.at[2]))
-    copies[2].start()
-    for copy in copies:
+    last = pltpu.make_async_copy(img, out_image, out_sem.at[2])
+
+    def compose(once, carry):
+        lane = lax.broadcasted_iota(jnp.int32, (8, 128), 1)
+        pieces = []
+        for first in range(0, CHIPS, HALF):
+            total, light = None, None
+            for i in range(first, first + HALF):
+                for c in range(2):
+                    tile = xr[c * CHIPS + i]
+                    color = jnp.where(lane < 96, tile, 0.0)
+                    passing = expand(tile, lane)
+                    total = color if total is None else total + light * color
+                    light = passing if light is None else light * passing
+            pieces.append((total, light))
+        while len(pieces) > 1:
+            pieces = [(near + light * far, light * light_far)
+                      for (near, light), (far, light_far) in zip(pieces[::2], pieces[1::2])]
+        total, light = pieces[0]
+        tile = jnp.where(lane < 96, total, 1.0 - light)
+        for g in range(8):
+            part = tile if g == 0 else pltpu.roll(tile, 128 - 16 * g, 1)
+            img[g // 2, pl.ds(8 * (g % 2), 8), :] = part[:, :16]
+        last.start()
+        return carry
+
+    lax.fori_loop(0, 1 + (lax.axis_index("depth") >> 6), compose, 0)
+    for copy in copies + [last]:
         copy.wait()
 
 
@@ -513,7 +537,7 @@
     dma = pltpu.SemaphoreType.DMA
     new, parts = pl.pallas_call(
         kernel,
-        out_shape=(pltpu.VMEM((2,) + field.shape, f32), pltpu.VMEM((3 * CHIPS, 8, 128), f32)),
+        out_shape=(pltpu.VMEM((2,) + field.shape, f32), pltpu.VMEM((2 * CHIPS, 8, 128), f32)),
         in_specs=[any_ref] * 6,
         out_specs=(pl.BlockSpec(memory_space=pltpu.VMEM),) * 2,
         scratch_shapes=[
@@ -529,7 +553,7 @@
             pltpu.VMEM((2, 2, LAYERS, CT, 128), f32),
             pltpu.VMEM((2, 2, LAYERS, CT, 128), f32),
             pltpu.VMEM((2, 2, LAYERS, CT, 128), f32),
-            pltpu.VMEM((2, 2, 2, CT, 128), f32),
+            pltpu.VMEM((2, 1, 2, CT, 128), f32),
             pltpu.VMEM((2, 2, 2, CT, 128), f32),
             pltpu.VMEM((4, CT * 16, 128), f32),
             pltpu.VMEM((CT * 8, 8, 128), f32),
@@ -540,7 +564,7 @@
             dma((6,)),
             dma((2,)), dma((2,)), dma((2,)), dma((2, 2)),
             dma((2,)), dma((2,)), dma((2,)), dma((2,)),
-            dma((2,)), dma((2,)), dma((2,)), dma((2,)),
+            dma((2,)), dma((2,)), dma, dma, dma((2,)), dma((2,)),
             dma((2,)), dma((2,)), dma, dma,
             pltpu.SemaphoreType.REGULAR, pltpu.SemaphoreType.REGULAR,
         ],

time: 23.6 us -> 23.3 us (0.987)
  Pallas kernels: 22.8 us -> 22.5 us
    pallas_call x1, Pallas kernels: 21.8 us -> 21.5 us  [body(): pl.pallas_call(kernel, out_shape=(pltpu.VMEM((2,) + field.shape, f32), pl...]
where the time goes in v6:
time: 23.3 us; the launch traced here: 23.2 us
  Pallas kernels  22.5 us (97%)
  between operations  0.64 us (3%)
    pallas_call x1, Pallas kernels, body(): pl.pallas_call(kernel, out_shape=(pltpu.VMEM((2,) + field.shape, f32), pl...  21.5 us
    pallas_call x1, Pallas kernels, body(): pl.pallas_call(finish, out_shape=(field, field, jax.ShapeDtypeStruct((4,...  1.01 us

profile of v6, /device:TPU:1, one launch (start us, length us, event | category | flops | bytes accessed | tf_op | source)
XLA Modules:
  0.0 23.2 jit_solution(11580319514927378175)
XLA Ops:
  0.6 21.5 %shard_map.85 = (f32[2,4,16,1024]{3,2,1,0:T(8,128)S(1)}, f32[64,8,128]{2,1,0:T(8,128)S(1)}) custom-call(f32[3,3]{1,0:T(4,128)} %palette.1, f32[4,16,1024]{2,1,0:T(8,128)} %S.1, f32[4,16,1024]{2,1,0:T(8,128)} %C.1, f32[4,16,1024]{2,1,0:T(8,128)} %F.1, f32[4,16,1024]{2,1,0:T(8,128)} %K.1, f32[4,16,1024]{2,1,0:T(8,128)} %E.1), custom_call_target="tpu_custom_call" | custom-call | tf_op jit(solution)/shard_map/pallas_call | solution.py:538
  22.1 1.0 %shard_map.86 = (f32[4,16,1024]{2,1,0:T(8,128)}, f32[4,16,1024]{2,1,0:T(8,128)}, f32[4,16,16]{2,1,0:T(8,128)}) custom-call(f32[2,4,16,1024]{3,2,1,0:T(8,128)S(1)} %get-tuple-element.5.new, f32[64,8,128]{2,1,0:T(8,128)S(1)} %get-tuple-element.6.xr), custom_call_target="tpu_custom_call" | custom-call | tf_op jit(solution)/shard_map/pallas_call | solution.py:573

commit v7 on v6

--- a/solution.py
+++ b/solution.py
@@ -20,8 +20,8 @@
 FIRST = 8
 GROUP = 4
 HALF = CT // 2
-COLLECTORS = (9, (Y // 2) * X + X // 2)
-DIRECT = ((4, 2), (4, 1), (4, 3), (3, 2), (5, 2), (6, 2))
+COLLECTORS = (10, (Y // 2) * X + X // 2)
+DIRECT = ((4, 2), (4, 1), (4, 3), (3, 2), (5, 2))
 TILES = CHIPS - 1 + len(DIRECT)
 
 
@@ -49,8 +49,8 @@
 
 def kernel(palette, S, C, F, K, E, new, xr,
            s0, s1, fv, kv, ev, h0, ph, ps, r0, r1, rs0, rs1, eg, dg, mid, flat, t0, cr, x0, pal,
-           load_sem, h_send, h_recv, p_send, p_recv, r0_send, r0_recv, r1_send, r1_recv,
-           e_send, e_recv, g_send, g_recv, s_send, s_recv, c_send, c_recv, x_send, x_recv, everyone, ready):
+           load_sem, sent, h_recv, p_recv, r0_recv, r1_recv,
+           e_recv, g_recv, s_recv, c_recv, x_send, x_recv, everyone, ready):
     d = lax.axis_index("depth")
     z = lax.axis_index("rows")
     core = d & 1
@@ -113,13 +113,16 @@
     def _():
         signal(ready, d, zdown)
 
-    @pl.when(collects)
-    def _():
-        def tell(i, carry):
+    def tell():
+        def one(i, carry):
             signal(everyone, 2 * ((chip + i) & (CHIPS - 1)) + core, z)
             return carry
 
-        lax.fori_loop(1, CHIPS, tell, 0)
+        lax.fori_loop(1, CHIPS, one, 0)
+
+    @pl.when(collects & (z == 0))
+    def _():
+        tell()
 
     zero = jnp.zeros((8, 128), jnp.float32)
     for sp in range(2):
@@ -167,27 +170,27 @@
         target = up if side == 0 else down
         if kind == "h":
             src = (S, C)[sp].at[LAYERS - 1 if side == 0 else 0]
-            return remote(src, h0.at[side, sp], h_send.at[side], h_recv.at[side], target, z)
+            return remote(src, h0.at[side, sp], sent, h_recv.at[side], target, z)
         if kind == "both":
-            return remote(h0.at[side], h0.at[side], h_send.at[side], h_recv.at[side], target, z)
+            return remote(h0.at[side], h0.at[side], sent, h_recv.at[side], target, z)
         if kind == "halves":
-            return remote(ps.at[side], ph.at[side], p_send.at[side], p_recv.at[side, 0], target, z)
+            return remote(ps.at[side], ph.at[side], sent, p_recv.at[side, 0], target, z)
         if kind == "p":
             half = sp
-            return remote(ps.at[side, half], ph.at[side, half], p_send.at[side], p_recv.at[side, half], target, z)
+            return remote(ps.at[side, half], ph.at[side, half], sent, p_recv.at[side, half], target, z)
         if kind == "straight":
             return remote(rs0.at[1, :, LAYERS - 1 if side == 0 else 0], dg.at[side, 1],
-                          s_send.at[side], s_recv.at[side], target, zdown)
+                          sent, s_recv.at[side], target, zdown)
         return remote(rs0.at[0:1, :, LAYERS - 1 if side == 0 else 0], eg.at[side],
-                      e_send.at[side], e_recv.at[side], target, z)
+                      sent, e_recv.at[side], target, z)
 
     def row_copy(kind, side):
         target = zup if side == 0 else zdown
         if kind == "0":
-            return remote(rs0.at[side], r0.at[side], r0_send.at[side], r0_recv.at[side], d, target)
+            return remote(rs0.at[side], r0.at[side], sent, r0_recv.at[side], d, target)
         if kind == "corner":
-            return remote(eg.at[:, 0], dg.at[:, 0], g_send, g_recv, d, target)
-        return remote(rs1.at[side], r1.at[side], r1_send.at[side], r1_recv.at[side], d, target)
+            return remote(eg.at[:, 0], dg.at[:, 0], sent, g_recv, d, target)
+        return remote(rs1.at[side], r1.at[side], sent, r1_recv.at[side], d, target)
 
     to = ("hi", "lo")
     source = ("lo", "hi")
@@ -214,6 +217,10 @@
     for side in range(2):
         each(to[side], [depth_copy("edge", side, 0)] + [depth_copy("h", side, sp) for sp in range(2)], "start")
     each("zlo", [row_copy("0", 1)], "start")
+
+    @pl.when(collects & (z > 0))
+    def _():
+        tell()
 
     with mark("w_loadfk"):
         f_load.wait()
@@ -421,7 +428,7 @@
 
     def core_copy(g):
         some = pl.ds(g * HALF * X, HALF * X)
-        return remote(t0.at[1 - core, some], cr.at[some], c_send.at[g], c_recv.at[g], partner, z)
+        return remote(t0.at[1 - core, some], cr.at[some], sent, c_recv.at[g], partner, z)
 
     def ends(g):
         with mark(f"w_p{g}"):
@@ -562,10 +569,10 @@
             pltpu.VMEM((CHIPS, 8, 128), f32),
             pltpu.SMEM((3, 3), f32),
             dma((6,)),
-            dma((2,)), dma((2,)), dma((2,)), dma((2, 2)),
-            dma((2,)), dma((2,)), dma((2,)), dma((2,)),
-            dma((2,)), dma((2,)), dma, dma, dma((2,)), dma((2,)),
-            dma((2,)), dma((2,)), dma, dma,
+            dma, dma((2,)), dma((2, 2)),
+            dma((2,)), dma((2,)),
+            dma((2,)), dma, dma((2,)),
+            dma((2,)), dma, dma,
             pltpu.SemaphoreType.REGULAR, pltpu.SemaphoreType.REGULAR,
         ],
         compiler_params=pltpu.CompilerParams(collective_id=0, has_side_effects=True),

time: 23.3 us -> 22.7 us (0.974)
  Pallas kernels: 22.5 us -> 21.9 us
    pallas_call x1, Pallas kernels: 21.5 us -> 20.9 us  [body(): pl.pallas_call(kernel, out_shape=(pltpu.VMEM((2,) + field.shape, f32), pl...]
where the time goes in v7:
time: 22.7 us; the launch traced here: 22.5 us
  Pallas kernels  21.9 us (96%)
  between operations  0.64 us (3%)
    pallas_call x1, Pallas kernels, body(): pl.pallas_call(kernel, out_shape=(pltpu.VMEM((2,) + field.shape, f32), pl...  20.9 us
    pallas_call x1, Pallas kernels, body(): pl.pallas_call(finish, out_shape=(field, field, jax.ShapeDtypeStruct((4,...  1.01 us

profile of v7, /device:TPU:1, one launch (start us, length us, event | category | flops | bytes accessed | tf_op | source)
XLA Modules:
  0.0 22.5 jit_solution(15520020944422398568)
XLA Ops:
  0.6 20.9 %shard_map.85 = (f32[2,4,16,1024]{3,2,1,0:T(8,128)S(1)}, f32[64,8,128]{2,1,0:T(8,128)S(1)}) custom-call(f32[3,3]{1,0:T(4,128)} %palette.1, f32[4,16,1024]{2,1,0:T(8,128)} %S.1, f32[4,16,1024]{2,1,0:T(8,128)} %C.1, f32[4,16,1024]{2,1,0:T(8,128)} %F.1, f32[4,16,1024]{2,1,0:T(8,128)} %K.1, f32[4,16,1024]{2,1,0:T(8,128)} %E.1), custom_call_target="tpu_custom_call" | custom-call | tf_op jit(solution)/shard_map/pallas_call | solution.py:545
  21.5 1.0 %shard_map.86 = (f32[4,16,1024]{2,1,0:T(8,128)}, f32[4,16,1024]{2,1,0:T(8,128)}, f32[4,16,16]{2,1,0:T(8,128)}) custom-call(f32[2,4,16,1024]{3,2,1,0:T(8,128)S(1)} %get-tuple-element.5.new, f32[64,8,128]{2,1,0:T(8,128)S(1)} %get-tuple-element.6.xr), custom_call_target="tpu_custom_call" | custom-call | tf_op jit(solution)/shard_map/pallas_call | solution.py:580

commit v8 on v7

--- a/solution.py
+++ b/solution.py
@@ -22,6 +22,7 @@
 HALF = CT // 2
 COLLECTORS = (10, (Y // 2) * X + X // 2)
 DIRECT = ((4, 2), (4, 1), (4, 3), (3, 2), (5, 2))
+SEAM = 4
 TILES = CHIPS - 1 + len(DIRECT)
 
 
@@ -106,24 +107,6 @@
     e_load.start()
     pal_load.start()
 
-    with mark("w_barrier"):
-        pl.semaphore_wait(barrier, sum(jnp.where(has[flag], 1, 0) for flag in ("lo", "hi", "zlo", "above_lo", "above_hi")) + jnp.where(collects, DEPTHS - 1, 0))
-
-    @pl.when(has["zlo"])
-    def _():
-        signal(ready, d, zdown)
-
-    def tell():
-        def one(i, carry):
-            signal(everyone, 2 * ((chip + i) & (CHIPS - 1)) + core, z)
-            return carry
-
-        lax.fori_loop(1, CHIPS, one, 0)
-
-    @pl.when(collects & (z == 0))
-    def _():
-        tell()
-
     zero = jnp.zeros((8, 128), jnp.float32)
     for sp in range(2):
         for layer in range(LAYERS):
@@ -133,99 +116,6 @@
                         buf[sp, layer, pl.ds(t * TILE + FIRST + 8 * rb, 8), :] = zero
             for row in (FIRST - 1, FIRST + 16):
                 s0[sp, layer, pl.ds(TILE + row, CT, stride=TILE), :] = zero
-    clear = jnp.where(lax.broadcasted_iota(jnp.int32, (8, 128), 1) < 96, 0.0, 1.0)
-    for away in range(Y):
-        for across in range(X):
-            if (away, across) not in DIRECT:
-                xr[CHIPS + ((y - away) & (Y - 1)) * X + ((x - across) & (X - 1))] = clear
-    for side, flag in ((0, "lo"), (1, "hi")):
-        @pl.when(jnp.logical_not(has[flag]))
-        def _(side=side):
-            for sp in range(2):
-                eg[side, 0, sp] = zero
-                dg[side, 1, sp] = zero
-
-                def fill(i, carry):
-                    h0[side, sp, :, pl.ds(i * 128, 128)] = jnp.zeros((16, 128), jnp.float32)
-                    ph[side, i // HALF, sp, pl.ds((i % HALF) * 16, 16), :] = jnp.zeros((16, 128), jnp.float32)
-                    return carry
-
-                lax.fori_loop(0, CT, fill, 0)
-    for side, flag in ((0, "zlo"), (1, "zhi")):
-        @pl.when(jnp.logical_not(has[flag]))
-        def _(side=side):
-            for sp in range(2):
-                for layer in range(LAYERS):
-                    r0[side, sp, layer] = zero
-                    r1[side, sp, layer] = zero
-                for depthside in range(2):
-                    dg[depthside, side, sp] = zero
-
-    def remote(src, dst, send, recv, depth, row):
-        return pltpu.make_async_remote_copy(
-            src_ref=src, dst_ref=dst, send_sem=send, recv_sem=recv,
-            device_id=(depth, row), device_id_type=MESH)
-
-    def depth_copy(kind, side, sp):
-        target = up if side == 0 else down
-        if kind == "h":
-            src = (S, C)[sp].at[LAYERS - 1 if side == 0 else 0]
-            return remote(src, h0.at[side, sp], sent, h_recv.at[side], target, z)
-        if kind == "both":
-            return remote(h0.at[side], h0.at[side], sent, h_recv.at[side], target, z)
-        if kind == "halves":
-            return remote(ps.at[side], ph.at[side], sent, p_recv.at[side, 0], target, z)
-        if kind == "p":
-            half = sp
-            return remote(ps.at[side, half], ph.at[side, half], sent, p_recv.at[side, half], target, z)
-        if kind == "straight":
-            return remote(rs0.at[1, :, LAYERS - 1 if side == 0 else 0], dg.at[side, 1],
-                          sent, s_recv.at[side], target, zdown)
-        return remote(rs0.at[0:1, :, LAYERS - 1 if side == 0 else 0], eg.at[side],
-                      sent, e_recv.at[side], target, z)
-
-    def row_copy(kind, side):
-        target = zup if side == 0 else zdown
-        if kind == "0":
-            return remote(rs0.at[side], r0.at[side], sent, r0_recv.at[side], d, target)
-        if kind == "corner":
-            return remote(eg.at[:, 0], dg.at[:, 0], sent, g_recv, d, target)
-        return remote(rs1.at[side], r1.at[side], sent, r1_recv.at[side], d, target)
-
-    to = ("hi", "lo")
-    source = ("lo", "hi")
-    zto = ("zhi", "zlo")
-    zsource = ("zlo", "zhi")
-
-    def each(flag, copies, what):
-        @pl.when(has[flag])
-        def _():
-            for copy in copies:
-                getattr(copy, what)()
-
-    with mark("w_load"):
-        for sp in range(2):
-            whole = s0.at[sp, :, pl.ds(0, CT * 16), :]
-            pltpu.make_async_copy(whole, whole, load_sem.at[sp]).wait()
-    for side in range(2):
-        row = TILE + FIRST + (15 if side == 0 else 0)
-        for sp in range(2):
-            for layer in range(LAYERS):
-                rs0[side, sp, layer] = s0[sp, layer, pl.ds(row, CT, stride=TILE), :]
-    for side in range(2):
-        each("above_" + to[side], [depth_copy("straight", side, 0)], "start")
-    for side in range(2):
-        each(to[side], [depth_copy("edge", side, 0)] + [depth_copy("h", side, sp) for sp in range(2)], "start")
-    each("zlo", [row_copy("0", 1)], "start")
-
-    @pl.when(collects & (z > 0))
-    def _():
-        tell()
-
-    with mark("w_loadfk"):
-        f_load.wait()
-        k_load.wait()
-
     lane = lax.broadcasted_iota(jnp.int32, (8, 128), 1)
 
     def in_groups(step):
@@ -290,12 +180,143 @@
 
         in_groups(body)
 
-    with mark("first03"):
+    early = (z == SEAM) & (collects | ((x == 0) & (core == 0) & (y > 0)) | ((x == X - 1) & (core == 1) & (y < Y // 2)))
+    later = jnp.logical_not(early)
+
+    def fields_loaded():
+        with mark("w_load"):
+            for sp in range(2):
+                whole = s0.at[sp, :, pl.ds(0, CT * 16), :]
+                pltpu.make_async_copy(whole, whole, load_sem.at[sp]).wait()
+
+    def rates_loaded():
+        with mark("w_loadfk"):
+            f_load.wait()
+            k_load.wait()
+
+
+    @pl.when(early)
+    def _():
+        fields_loaded()
+        rates_loaded()
         first((0, LAYERS - 1))
+        first(range(1, LAYERS - 1))
+
+    with mark("w_barrier"):
+        pl.semaphore_wait(barrier, sum(jnp.where(has[flag], 1, 0) for flag in ("lo", "hi", "zlo", "above_lo", "above_hi")) + jnp.where(collects, DEPTHS - 1, 0))
+
+    @pl.when(has["zlo"])
+    def _():
+        signal(ready, d, zdown)
+
+    def tell():
+        def one(i, carry):
+            signal(everyone, 2 * ((chip + i) & (CHIPS - 1)) + core, z)
+            return carry
+
+        lax.fori_loop(1, CHIPS, one, 0)
+
+    @pl.when(collects & (z == 0))
+    def _():
+        tell()
+
+    clear = jnp.where(lax.broadcasted_iota(jnp.int32, (8, 128), 1) < 96, 0.0, 1.0)
+    for away in range(Y):
+        for across in range(X):
+            if (away, across) not in DIRECT:
+                xr[CHIPS + ((y - away) & (Y - 1)) * X + ((x - across) & (X - 1))] = clear
+    for side, flag in ((0, "lo"), (1, "hi")):
+        @pl.when(jnp.logical_not(has[flag]))
+        def _(side=side):
+            for sp in range(2):
+                eg[side, 0, sp] = zero
+                dg[side, 1, sp] = zero
+
+                def fill(i, carry):
+                    h0[side, sp, :, pl.ds(i * 128, 128)] = jnp.zeros((16, 128), jnp.float32)
+                    ph[side, i // HALF, sp, pl.ds((i % HALF) * 16, 16), :] = jnp.zeros((16, 128), jnp.float32)
+                    return carry
+
+                lax.fori_loop(0, CT, fill, 0)
+    for side, flag in ((0, "zlo"), (1, "zhi")):
+        @pl.when(jnp.logical_not(has[flag]))
+        def _(side=side):
+            for sp in range(2):
+                for layer in range(LAYERS):
+                    r0[side, sp, layer] = zero
+                    r1[side, sp, layer] = zero
+                for depthside in range(2):
+                    dg[depthside, side, sp] = zero
+
+    def remote(src, dst, send, recv, depth, row):
+        return pltpu.make_async_remote_copy(
+            src_ref=src, dst_ref=dst, send_sem=send, recv_sem=recv,
+            device_id=(depth, row), device_id_type=MESH)
+
+    def depth_copy(kind, side, sp):
+        target = up if side == 0 else down
+        if kind == "h":
+            src = (S, C)[sp].at[LAYERS - 1 if side == 0 else 0]
+            return remote(src, h0.at[side, sp], sent, h_recv.at[side], target, z)
+        if kind == "both":
+            return remote(h0.at[side], h0.at[side], sent, h_recv.at[side], target, z)
+        if kind == "halves":
+            return remote(ps.at[side], ph.at[side], sent, p_recv.at[side, 0], target, z)
+        if kind == "p":
+            half = sp
+            return remote(ps.at[side, half], ph.at[side, half], sent, p_recv.at[side, half], target, z)
+        if kind == "straight":
+            return remote(rs0.at[1, :, LAYERS - 1 if side == 0 else 0], dg.at[side, 1],
+                          sent, s_recv.at[side], target, zdown)
+        return remote(rs0.at[0:1, :, LAYERS - 1 if side == 0 else 0], eg.at[side],
+                      sent, e_recv.at[side], target, z)
+
+    def row_copy(kind, side):
+        target = zup if side == 0 else zdown
+        if kind == "0":
+            return remote(rs0.at[side], r0.at[side], sent, r0_recv.at[side], d, target)
+        if kind == "corner":
+            return remote(eg.at[:, 0], dg.at[:, 0], sent, g_recv, d, target)
+        return remote(rs1.at[side], r1.at[side], sent, r1_recv.at[side], d, target)
+
+    to = ("hi", "lo")
+    source = ("lo", "hi")
+    zto = ("zhi", "zlo")
+    zsource = ("zlo", "zhi")
+
+    def each(flag, copies, what):
+        @pl.when(has[flag])
+        def _():
+            for copy in copies:
+                getattr(copy, what)()
+
+    pl.when(later)(fields_loaded)
+    for side in range(2):
+        row = TILE + FIRST + (15 if side == 0 else 0)
+        for sp in range(2):
+            for layer in range(LAYERS):
+                rs0[side, sp, layer] = s0[sp, layer, pl.ds(row, CT, stride=TILE), :]
+    for side in range(2):
+        each("above_" + to[side], [depth_copy("straight", side, 0)], "start")
+    for side in range(2):
+        each(to[side], [depth_copy("edge", side, 0)] + [depth_copy("h", side, sp) for sp in range(2)], "start")
+    each("zlo", [row_copy("0", 1)], "start")
+
+    @pl.when(collects & (z > 0))
+    def _():
+        tell()
+
+    @pl.when(later)
+    def _():
+        rates_loaded()
+        first((0, LAYERS - 1))
+
     for side in range(2):
         each(to[side], [depth_copy("p", side, half) for half in range(2)], "start")
-    with mark("first12"):
+    @pl.when(later)
+    def _():
         first(range(1, LAYERS - 1))
+
     for side in range(2):
         row = TILE + FIRST + (15 if side == 0 else 0)
         for sp in range(2):

time: 22.7 us -> 22.7 us (level)
  no operation moved by 1% of the time
where the time goes in v8:
time: 22.7 us; the launch traced here: 22.5 us
  Pallas kernels  21.9 us (96%)
  between operations  0.64 us (3%)
    pallas_call x1, Pallas kernels, body(): pl.pallas_call(kernel, out_shape=(pltpu.VMEM((2,) + field.shape, f32), pl...  20.9 us
    pallas_call x1, Pallas kernels, body(): pl.pallas_call(finish, out_shape=(field, field, jax.ShapeDtypeStruct((4,...  1.01 us

profile of v8, /device:TPU:1, one launch (start us, length us, event | category | flops | bytes accessed | tf_op | source)
XLA Modules:
  0.0 22.5 jit_solution(17304125416220324705)
XLA Ops:
  0.6 20.9 %shard_map.85 = (f32[2,4,16,1024]{3,2,1,0:T(8,128)S(1)}, f32[64,8,128]{2,1,0:T(8,128)S(1)}) custom-call(f32[3,3]{1,0:T(4,128)} %palette.1, f32[4,16,1024]{2,1,0:T(8,128)} %S.1, f32[4,16,1024]{2,1,0:T(8,128)} %C.1, f32[4,16,1024]{2,1,0:T(8,128)} %F.1, f32[4,16,1024]{2,1,0:T(8,128)} %K.1, f32[4,16,1024]{2,1,0:T(8,128)} %E.1), custom_call_target="tpu_custom_call" | custom-call | tf_op jit(solution)/shard_map/pallas_call | solution.py:566
  21.5 1.0 %shard_map.86 = (f32[4,16,1024]{2,1,0:T(8,128)}, f32[4,16,1024]{2,1,0:T(8,128)}, f32[4,16,16]{2,1,0:T(8,128)}) custom-call(f32[2,4,16,1024]{3,2,1,0:T(8,128)S(1)} %get-tuple-element.5.new, f32[64,8,128]{2,1,0:T(8,128)S(1)} %get-tuple-element.6.xr), custom_call_target="tpu_custom_call" | custom-call | tf_op jit(solution)/shard_map/pallas_call | solution.py:601

commit v9 on v8

--- a/solution.py
+++ b/solution.py
@@ -22,7 +22,6 @@
 HALF = CT // 2
 COLLECTORS = (10, (Y // 2) * X + X // 2)
 DIRECT = ((4, 2), (4, 1), (4, 3), (3, 2), (5, 2))
-SEAM = 4
 TILES = CHIPS - 1 + len(DIRECT)
 
 
@@ -51,7 +50,7 @@
 def kernel(palette, S, C, F, K, E, new, xr,
            s0, s1, fv, kv, ev, h0, ph, ps, r0, r1, rs0, rs1, eg, dg, mid, flat, t0, cr, x0, pal,
            load_sem, sent, h_recv, p_recv, r0_recv, r1_recv,
-           e_recv, g_recv, s_recv, c_recv, x_send, x_recv, everyone, ready):
+           e_recv, g_recv, s_recv, c_recv, x_recv, everyone, ready):
     d = lax.axis_index("depth")
     z = lax.axis_index("rows")
     core = d & 1
@@ -96,9 +95,9 @@
             pltpu.make_async_copy(
                 src.at[:, :, pl.ds(ct * 128, 128)],
                 s0.at[sp, :, pl.ds((ct + 1) * TILE + FIRST, 16), :],
-                load_sem.at[sp],
+                load_sem.at[0],
             ).start()
-    pal_load = pltpu.make_async_copy(palette, pal, load_sem.at[5])
+    pal_load = pltpu.make_async_copy(palette, pal, load_sem.at[1])
     f_load = pltpu.make_async_copy(F, fv, load_sem.at[2])
     k_load = pltpu.make_async_copy(K, kv, load_sem.at[3])
     e_load = pltpu.make_async_copy(E, ev, load_sem.at[4])
@@ -180,14 +179,13 @@
 
         in_groups(body)
 
-    early = (z == SEAM) & (collects | ((x == 0) & (core == 0) & (y > 0)) | ((x == X - 1) & (core == 1) & (y < Y // 2)))
+    early = (z > 0) & (collects | ((x == 0) & (core == 0) & (y > 0)) | ((x == X - 1) & (core == 1) & (y < Y // 2)))
     later = jnp.logical_not(early)
 
     def fields_loaded():
         with mark("w_load"):
-            for sp in range(2):
-                whole = s0.at[sp, :, pl.ds(0, CT * 16), :]
-                pltpu.make_async_copy(whole, whole, load_sem.at[sp]).wait()
+            whole = s0.at[:, :, pl.ds(0, CT * 16), :]
+            pltpu.make_async_copy(whole, whole, load_sem.at[0]).wait()
 
     def rates_loaded():
         with mark("w_loadfk"):
@@ -480,7 +478,7 @@
             if place // HALF == g:
                 yy, xx = (y + away) & (Y - 1), (x + across) & (X - 1)
                 for c in range(2):
-                    remote(t0.at[c, place * X + xx], xr.at[CHIPS * core + chip], x_send, x_recv, at(yy, xx, c), z).start()
+                    remote(t0.at[c, place * X + xx], xr.at[CHIPS * core + chip], sent, x_recv, at(yy, xx, c), z).start()
 
     with mark("w_everyone"):
         @pl.when(jnp.logical_not(collects))
@@ -493,7 +491,7 @@
 
     def chip_copy(place, away, across):
         xx = (x + across) & (X - 1)
-        return remote(x0.at[place * X + xx], xr.at[chip], x_send, x_recv, at((y + away) & (Y - 1), xx, core), z)
+        return remote(x0.at[place * X + xx], xr.at[chip], sent, x_recv, at((y + away) & (Y - 1), xx, core), z)
 
     def merge(g):
         core_copy(g).wait_recv()
@@ -519,7 +517,7 @@
     arrived = xr.at[pl.ds(0, TILES)]
     with mark("w_xy"):
         pltpu.make_async_copy(arrived, arrived, x_recv).wait()
-    pltpu.make_async_copy(arrived, arrived, x_send).wait()
+    pltpu.make_async_copy(arrived, arrived, sent).wait()
 
 
 def finish(new, xr, out_s, out_c, out_image, img, out_sem):
@@ -575,7 +573,7 @@
             pltpu.VMEM((LAYERS, 16, CT * 128), f32),
             pltpu.VMEM((LAYERS, 16, CT * 128), f32),
             pltpu.VMEM((2, 2, 16, CT * 128), f32),
-            pltpu.VMEM((2, 2, 2, HALF * 16, 128), f32),
+            pltpu.VMEM((3, 2, 2, HALF * 16, 128), f32),
             pltpu.VMEM((2, 2, 2, HALF * 16, 128), f32),
             pltpu.VMEM((2, 2, LAYERS, CT, 128), f32),
             pltpu.VMEM((2, 2, LAYERS, CT, 128), f32),
@@ -589,11 +587,11 @@
             pltpu.VMEM((CHIPS, 8, 128), f32),
             pltpu.VMEM((CHIPS, 8, 128), f32),
             pltpu.SMEM((3, 3), f32),
-            dma((6,)),
+            dma((5,)),
             dma, dma((2,)), dma((2, 2)),
             dma((2,)), dma((2,)),
             dma((2,)), dma, dma((2,)),
-            dma((2,)), dma, dma,
+            dma((2,)), dma,
             pltpu.SemaphoreType.REGULAR, pltpu.SemaphoreType.REGULAR,
         ],
         compiler_params=pltpu.CompilerParams(collective_id=0, has_side_effects=True),

time: 22.7 us -> 22.7 us (level)
  no operation moved by 1% of the time
where the time goes in v9:
time: 22.7 us; the launch traced here: 22.5 us
  Pallas kernels  21.9 us (96%)
  between operations  0.64 us (3%)
    pallas_call x1, Pallas kernels, body(): pl.pallas_call(kernel, out_shape=(pltpu.VMEM((2,) + field.shape, f32), pl...  20.9 us
    pallas_call x1, Pallas kernels, body(): pl.pallas_call(finish, out_shape=(field, field, jax.ShapeDtypeStruct((4,...  1.01 us

profile of v9, /device:TPU:1, one launch (start us, length us, event | category | flops | bytes accessed | tf_op | source)
XLA Modules:
  0.0 22.5 jit_solution(14552907847272938867)
XLA Ops:
  0.6 20.9 %shard_map.85 = (f32[2,4,16,1024]{3,2,1,0:T(8,128)S(1)}, f32[64,8,128]{2,1,0:T(8,128)S(1)}) custom-call(f32[3,3]{1,0:T(4,128)} %palette.1, f32[4,16,1024]{2,1,0:T(8,128)} %S.1, f32[4,16,1024]{2,1,0:T(8,128)} %C.1, f32[4,16,1024]{2,1,0:T(8,128)} %F.1, f32[4,16,1024]{2,1,0:T(8,128)} %K.1, f32[4,16,1024]{2,1,0:T(8,128)} %E.1), custom_call_target="tpu_custom_call" | custom-call | tf_op jit(solution)/shard_map/pallas_call | solution.py:564
  21.5 1.0 %shard_map.86 = (f32[4,16,1024]{2,1,0:T(8,128)}, f32[4,16,1024]{2,1,0:T(8,128)}, f32[4,16,16]{2,1,0:T(8,128)}) custom-call(f32[2,4,16,1024]{3,2,1,0:T(8,128)S(1)} %get-tuple-element.5.new, f32[64,8,128]{2,1,0:T(8,128)S(1)} %get-tuple-element.6.xr), custom_call_target="tpu_custom_call" | custom-call | tf_op jit(solution)/shard_map/pallas_call | solution.py:599
